TPU v7x, 32 devices: a whole 2x2x4 slice. The times are simulated.
32 devices in a mesh: groups: 2 (over y), blk: 16 (over z, x, core).
Axes of the slice: x: 2, y: 2, z: 4, core: 2. Of those that a mesh axis runs over, the one named last changes fastest.
Arguments:
- queries: bfloat16 [2048, 2048], P(('groups', 'blk')), parts along dimension 0, may hold values from -48 to 48
- rotated_cache_keys: bfloat16 [16384, 256], P(('groups', 'blk')), parts along dimension 0, may hold values from -4 to 4
- stored_cache_values: bfloat16 [16384, 256], P(('groups', 'blk')), parts along dimension 0, may hold values from -5 to 5
- segment_new_keys: bfloat16 [2048, 256], P(('groups', 'blk')), parts along dimension 0, may hold values from -4 to 4
- segment_new_values: bfloat16 [2048, 256], P(('groups', 'blk')), parts along dimension 0, may hold values from -5 to 5
- block_ids: int32 [2048, 8], P(('groups', 'blk')), parts along dimension 0, may hold values from 0 to 15, all different within a row; in each aligned block of 64 rows (0 to 63, 64 to 127, ...) at most 40 rows name the same one
- residual_in: bfloat16 [2048, 1024], P(('groups', 'blk')), parts along dimension 0, may hold values from -3 to 3
- out_weight: bfloat16 [2048, 1024], replicated, may hold values from -1.5 to 1.5
- norm_gain: float32 [1024], replicated, may hold values from 0.25 to 1.75
- expert_ids: int32 [2048, 8], P(('groups', 'blk')), parts along dimension 0, may hold values from 0 to 15, all different within a row; in each aligned block of 64 rows (0 to 63, 64 to 127, ...) at most 48 rows name the same one
- gate_scores: float32 [2048, 8], P(('groups', 'blk')), parts along dimension 0, may hold values from 0.05 to 1
- w_gate: bfloat16 [16, 1024, 768], P('blk'), may hold values from -0.1875 to 0.1875
- w_up: bfloat16 [16, 1024, 768], P('blk'), may hold values from -0.1875 to 0.1875
- w_down: bfloat16 [16, 768, 1024], P('blk'), may hold values from -0.21875 to 0.21875
Outputs:
- layer_out: bfloat16 [2048, 1024], P(('groups', 'blk')), parts along dimension 0
There are 2 independent parts, one for each index of `groups`. A program takes and returns all parts, laid end to end along the dimension named above; an argument that names none is the same for every part. Nothing has to cross between parts.
Inputs may be any that keep to these rules, and one draw needn't show every extreme that they name: `block_ids`: each row names 8 different blocks. Among the rows of one device no block is named more than 40 times, and in some devices' rows some block is named exactly 40 times. `expert_ids`: each row names 8 different experts. Among the rows of one device no expert is named more than 48 times, and in some devices' rows some expert is named exactly 48 times.
All inputs are finite; a program needn't handle non-finite values.
Results may differ from a plain program's by a relative error of at most 0.0095.
Values may be sent and summed in bfloat16 or wider, within the bound.
A program may use at most 128 MiB of HBM per device.

v0:
```python
import jax
import jax.numpy as jnp
from jax import lax
from jax.sharding import PartitionSpec as P

QUERY_HEADS = 16
KEY_VALUE_HEADS = 2
HEAD_SIZE = 128
TOPB = 8
TOPE = 8


NORM_EPSILON = 1e-06


def partials(query_rows, key_rows, value_rows, causal):
    queries_per_cluster = QUERY_HEADS // KEY_VALUE_HEADS
    score_scale = HEAD_SIZE ** (-0.5)
    maxima = []
    totals = []
    outputs = []
    for head_cluster in range(KEY_VALUE_HEADS):
        offset = head_cluster * queries_per_cluster * HEAD_SIZE
        group_queries = query_rows[:, offset : offset + queries_per_cluster * HEAD_SIZE].reshape(
            -1, HEAD_SIZE
        )
        group_keys = key_rows[:, head_cluster * HEAD_SIZE : (head_cluster + 1) * HEAD_SIZE]
        group_values = value_rows[:, head_cluster * HEAD_SIZE : (head_cluster + 1) * HEAD_SIZE]
        scores = (
            lax.dot_general(
                group_queries,
                group_keys,
                (((1,), (1,)), ((), ())),
                preferred_element_type=jnp.float32,
            )
            * score_scale
        )
        if causal:
            owner_row = jnp.arange(group_queries.shape[0], dtype=jnp.int32) // queries_per_cluster
            key_place = jnp.arange(key_rows.shape[0], dtype=jnp.int32)
            scores = jnp.where(key_place[None, :] <= owner_row[:, None], scores, -jnp.inf)
        row_max = jnp.max(scores, axis=1)
        weights = jnp.exp(scores - row_max[:, None])
        maxima.append(row_max.reshape(-1, queries_per_cluster))
        totals.append(jnp.sum(weights, axis=1).reshape(-1, queries_per_cluster))
        mixed_rows = jnp.dot(
            weights.astype(jnp.bfloat16), group_values, preferred_element_type=jnp.float32
        )
        outputs.append(mixed_rows.reshape(-1, queries_per_cluster * HEAD_SIZE))
    return (
        jnp.concatenate(maxima, axis=1),
        jnp.concatenate(totals, axis=1),
        jnp.concatenate(outputs, axis=1),
    )


def bucket_slots(targets, capacity, parties):
    flat_targets = targets.reshape(-1)
    pair_count = flat_targets.shape[0]
    one_hot = (flat_targets[:, None] == jnp.arange(parties, dtype=jnp.int32)[None, :]).astype(
        jnp.int32
    )
    before = jnp.sum((jnp.cumsum(one_hot, axis=0) - one_hot) * one_hot, axis=1)
    slot_index = flat_targets * capacity + before
    filler = (
        jnp.full((parties * capacity,), pair_count, jnp.int32)
        .at[slot_index]
        .set(jnp.arange(pair_count, dtype=jnp.int32))
    )
    return (slot_index, filler)


def body(
    queries,
    rotated_cache_keys,
    stored_cache_values,
    segment_new_keys,
    segment_new_values,
    block_ids,
    residual_in,
    out_weight,
    norm_gain,
    expert_ids,
    gate_scores,
    w_gate,
    w_up,
    w_down,
):
    parties = lax.axis_size("blk")
    tok_count = queries.shape[0]
    capacity = tok_count * TOPB * 5 // (4 * parties)
    expert_capacity = tok_count * TOPE * 3 // (2 * parties)
    owner_slots, slot_pair = bucket_slots(block_ids, capacity, parties)
    pair_count = tok_count * TOPB
    occupied = slot_pair < pair_count
    source_token = jnp.minimum(slot_pair, pair_count - 1) // TOPB
    outgoing = jnp.where(
        occupied[:, None], queries[source_token], jnp.zeros((), queries.dtype)
    ).reshape(parties, capacity, QUERY_HEADS * HEAD_SIZE)
    arrived = lax.all_to_all(outgoing, "blk", split_axis=0, concat_axis=0, tiled=True)
    senders, items, row_width = arrived.shape
    far_max, far_total, far_out = partials(
        arrived.reshape(senders * items, row_width), rotated_cache_keys, stored_cache_values, False
    )
    back_max = lax.all_to_all(
        far_max.reshape(senders, items, QUERY_HEADS), "blk", split_axis=0, concat_axis=0, tiled=True
    )
    back_total = lax.all_to_all(
        far_total.reshape(senders, items, QUERY_HEADS),
        "blk",
        split_axis=0,
        concat_axis=0,
        tiled=True,
    )
    back_out = lax.all_to_all(
        far_out.astype(jnp.bfloat16).reshape(senders, items, row_width),
        "blk",
        split_axis=0,
        concat_axis=0,
        tiled=True,
    )
    local_row_maximum, local_denominator, local_output = partials(
        queries, segment_new_keys, segment_new_values, True
    )
    pair_max = back_max.reshape(-1, QUERY_HEADS)[owner_slots].reshape(tok_count, TOPB, QUERY_HEADS)
    pair_total = back_total.reshape(-1, QUERY_HEADS)[owner_slots].reshape(
        tok_count, TOPB, QUERY_HEADS
    )
    pair_out = back_out.reshape(-1, QUERY_HEADS * HEAD_SIZE)[owner_slots].reshape(
        tok_count, TOPB, QUERY_HEADS, HEAD_SIZE
    )
    ceiling = jnp.maximum(local_row_maximum, jnp.max(pair_max, axis=1))
    own_scale = jnp.exp(local_row_maximum - ceiling)
    pair_scale = jnp.exp(pair_max - ceiling[:, None, :])
    denominator = local_denominator * own_scale + jnp.sum(pair_total * pair_scale, axis=1)
    numerator = local_output.reshape(tok_count, QUERY_HEADS, HEAD_SIZE) * own_scale[
        :, :, None
    ] + jnp.einsum("tjh,tjhd->thd", pair_scale, pair_out, preferred_element_type=jnp.float32)
    attention = (
        (numerator / denominator[:, :, None])
        .reshape(tok_count, QUERY_HEADS * HEAD_SIZE)
        .astype(jnp.bfloat16)
    )
    hidden_state = residual_in.astype(jnp.float32) + jnp.dot(
        attention, out_weight, preferred_element_type=jnp.float32
    )
    normed = (
        hidden_state
        * lax.rsqrt(jnp.mean(hidden_state * hidden_state, axis=-1, keepdims=True) + NORM_EPSILON)
        * norm_gain
    ).astype(jnp.bfloat16)
    expert_slots, expert_pair = bucket_slots(expert_ids, expert_capacity, parties)
    expert_pairs = tok_count * TOPE
    expert_used = expert_pair < expert_pairs
    expert_token = jnp.minimum(expert_pair, expert_pairs - 1) // TOPE
    dispatched = jnp.where(
        expert_used[:, None], normed[expert_token], jnp.zeros((), normed.dtype)
    ).reshape(parties, expert_capacity, normed.shape[1])
    arrived = lax.all_to_all(dispatched, "blk", split_axis=0, concat_axis=0, tiled=True)
    flat_rows = arrived.reshape(-1, arrived.shape[2])
    gate_part = jnp.dot(flat_rows, w_gate[0], preferred_element_type=jnp.float32)
    up_part = jnp.dot(flat_rows, w_up[0], preferred_element_type=jnp.float32)
    inner = (jax.nn.silu(gate_part) * up_part).astype(jnp.bfloat16)
    expert_out = (
        jnp.dot(inner, w_down[0], preferred_element_type=jnp.float32)
        .astype(jnp.bfloat16)
        .reshape(arrived.shape)
    )
    returned = lax.all_to_all(expert_out, "blk", split_axis=0, concat_axis=0, tiled=True)
    gathered_rows = returned.reshape(-1, normed.shape[1])[expert_slots].reshape(
        tok_count, TOPE, normed.shape[1]
    )
    mixing = gate_scores / jnp.sum(gate_scores, axis=1, keepdims=True)
    mixture = jnp.einsum("tk,tkd->td", mixing, gathered_rows, preferred_element_type=jnp.float32)
    return (hidden_state + mixture).astype(jnp.bfloat16)


def solution(mesh):
    placed = (
        P(("groups", "blk"), None),
        P(("groups", "blk"), None),
        P(("groups", "blk"), None),
        P(("groups", "blk"), None),
        P(("groups", "blk"), None),
        P(("groups", "blk"), None),
        P(("groups", "blk"), None),
        P(),
        P(),
        P(("groups", "blk"), None),
        P(("groups", "blk"), None),
        P("blk", None, None),
        P("blk", None, None),
        P("blk", None, None),
    )
    return jax.shard_map(
        body, mesh=mesh, in_specs=placed, out_specs=P(("groups", "blk"), None), check_vma=False
    )
```

profile of v0, /device:TPU:0, one launch (start us, length us, event | category | flops | bytes accessed | tf_op | source)
XLA Modules:
  0.0 308.2 jit_solution(5231597037997804013)
XLA Ops:
  3.5 2.4 scatter_custom_fusion
  6.1 4.1 %gather_fusion = bf16[640,2048]{1,0:T(8,128)(2,1)} fusion(bf16[64,2048]{1,0:T(8,128)(2,1)S(1)} %copy-done.1, s32[1024]{0:T(1024)S(1)} %pad_clamp_fusion.3), kind=kCustom, calls=%fused_computation | custom fusion | bytes 5245440 | tf_op jit(solution)/shard_map/gather | solution.py:98
  12.2 65.6 %all_to_all.30 = bf16[16,40,2048]{2,1,0:T(8,128)(2,1)S(1)} all-to-all(bf16[16,40,2048]{2,1,0:T(8,128)(2,1)S(1)} %broadcast_select_fusion), channel_id=1, replica_groups=mesh['groups'=2,'blk'=16] {'blk'}, dimensions={0} | all-to-all | bytes 5242880 | tf_op jit(solution)/shard_map/all_to_all | solution.py:100
  82.9 5.5 %multiply_reduce_fusion = (f32[5120]{0:T(1024)S(1)}, f32[5120,512]{0,1:T(8,128)}) fusion(bf16[5120,128]{1,0:T(8,128)(2,1)S(1)} %reshape.315, bf16[512,256]{1,0:T(8,128)(2,1)S(1)} %copy-done.11), kind=kOutput, calls=%fused_computation.10 | convolution fusion | flops 676326400 | bytes 11948032 | tf_op jit(solution)/shard_map/dot_general | solution.py:30
  88.6 5.9 %fusion.2 = f32[5120]{0:T(1024)S(1)} fusion(f32[5120,512]{0,1:T(8,128)} %get-tuple-element.12, f32[5120]{0:T(1024)S(1)} %get-tuple-element.11), kind=kLoop, calls=%fused_computation.14 | loop fusion | flops 7859200 | bytes 10526720 | tf_op jit(solution)/shard_map/reduce_sum | solution.py:45
  95.6 3.3 %convolution_convert_fusion = bf16[5120,128]{1,0:T(8,128)(2,1)S(1)} fusion(f32[5120,512]{0,1:T(8,128)S(1)} %copy-done.2, f32[5120]{0:T(1024)S(1)} %get-tuple-element.11, bf16[512,256]{1,0:T(8,128)(2,1)} %param.16), kind=kOutput, calls=%fused_computation.16 | convolution fusion | flops 679608320 | bytes 11948032 | tf_op jit(solution)/shard_map/dot_general | solution.py:46
  102.7 3.3 %convolution_convert_fusion.1 = bf16[5120,128]{1,0:T(8,128)(2,1)} fusion(f32[5120,512]{0,1:T(8,128)S(1)} %get-tuple-element.14, f32[5120]{0:T(1024)S(1)} %get-tuple-element.13, bf16[512,256]{1,0:T(8,128)(2,1)S(1)} %copy-done.13), kind=kOutput, calls=%fused_computation.17 | convolution fusion | flops 679608320 | bytes 11948032 | tf_op jit(solution)/shard_map/dot_general | solution.py:46
  109.5 3.4 %concatenate.76 = bf16[16,40,1024]{2,1,0:T(8,128)(2,1)} reshape(bf16[5120,128]{1,0:T(8,128)(2,1)} %convolution_convert_fusion.1) | data formatting | bytes 2621440 | tf_op jit(solution)/shard_map/concatenate | solution.py:53
  115.3 5.2 %all-to-all-start.1 = ((f32[16,1,640]{2,1,0:T(1,128)}), f32[16,1,640]{2,1,0:T(1,128)}, u32[]{:S(2)}, u32[]{:S(2)}) async-start(f32[16,1,640]{2,1,0:T(1,128)} %reshape.403), calls=%async_computation.1 | async-start | bytes 81920 | tf_op jit(solution)/shard_map/all_to_all | solution.py:105
  123.8 3.4 %all-to-all-done.1 = f32[16,1,640]{2,1,0:T(1,128)} async-done(((f32[16,1,640]{2,1,0:T(1,128)}), f32[16,1,640]{2,1,0:T(1,128)}, u32[]{:S(2)}, u32[]{:S(2)}) %all-to-all-start.1) | async-done | bytes 40992 | tf_op jit(solution)/shard_map/all_to_all | solution.py:105
  127.3 3.5 %all-to-all-start.3 = ((f32[16,1,640]{2,1,0:T(1,128)}), f32[16,1,640]{2,1,0:T(1,128)S(1)}, u32[]{:S(2)}, u32[]{:S(2)}) async-start(f32[16,1,640]{2,1,0:T(1,128)} %reshape.405), calls=%async_computation.3 | async-start | bytes 81920 | tf_op jit(solution)/shard_map/all_to_all | solution.py:108
  130.8 3.1 %pad_maximum_fusion = bf16[16,40,2048]{2,1,0:T(8,128)(2,1)} fusion(bf16[16,40,1024]{2,1,0:T(8,128)(2,1)S(1)} %copy-done.4, bf16[16,40,1024]{2,1,0:T(8,128)(2,1)} %concatenate.76), kind=kLoop, calls=%fused_computation.22 | loop fusion | flops 5242880 | bytes 5242880 | tf_op jit(solution)/shard_map/concatenate | solution.py:53
  133.9 3.6 %all-to-all-done.3 = f32[16,1,640]{2,1,0:T(1,128)S(1)} async-done(((f32[16,1,640]{2,1,0:T(1,128)}), f32[16,1,640]{2,1,0:T(1,128)S(1)}, u32[]{:S(2)}, u32[]{:S(2)}) %all-to-all-start.3) | async-done | bytes 40992 | tf_op jit(solution)/shard_map/all_to_all | solution.py:108
  137.4 4.4 %all-to-all-start.2 = ((bf16[16,40,2048]{2,1,0:T(8,128)(2,1)}), bf16[16,40,2048]{2,1,0:T(8,128)(2,1)}, u32[]{:S(2)}, u32[]{:S(2)}) async-start(bf16[16,40,2048]{2,1,0:T(8,128)(2,1)} %pad_maximum_fusion), calls=%async_computation.2 | async-start | bytes 5242880 | tf_op jit(solution)/shard_map/all_to_all | solution.py:115
  156.5 35.5 %all-to-all-done.2 = bf16[16,40,2048]{2,1,0:T(8,128)(2,1)} async-done(((bf16[16,40,2048]{2,1,0:T(8,128)(2,1)}), bf16[16,40,2048]{2,1,0:T(8,128)(2,1)}, u32[]{:S(2)}, u32[]{:S(2)}) %all-to-all-start.2) | async-done | bytes 2621472 | tf_op jit(solution)/shard_map/all_to_all | solution.py:115
  192.0 7.3 %gather_fusion.2 = bf16[512,2048]{1,0:T(8,128)(2,1)} fusion(bf16[640,2048]{1,0:T(8,128)(2,1)} %bitcast.10, s32[1024]{0:T(1024)S(1)} %pad_clamp_fusion.2), kind=kCustom, calls=%fused_computation.2 | custom fusion | bytes 4196352 | tf_op jit(solution)/shard_map/gather | solution.py:129
  199.3 3.0 fusion.10
  204.4 2.8 gather_fusion.4
  207.4 49.1 %all_to_all.31 = bf16[16,48,1024]{2,1,0:T(8,128)(2,1)S(1)} all-to-all(bf16[16,48,1024]{2,1,0:T(8,128)(2,1)S(1)} %broadcast_select_fusion.1), channel_id=1, replica_groups=mesh['groups'=2,'blk'=16] {'blk'}, dimensions={0} | all-to-all | bytes 3145728 | tf_op jit(solution)/shard_map/all_to_all | solution.py:159
  256.6 2.8 fusion.14
  259.4 6.6 %convolution_convert_fusion.2 = bf16[768,1024]{1,0:T(8,128)(2,1)} fusion(bf16[1,768,1024]{2,1,0:T(8,128)(2,1)S(1)} %copy-done, f32[768,768]{1,0:T(8,128)} %fusion.14, bf16[768,1024]{1,0:T(8,128)(2,1)S(1)} %bitcast.126, bf16[1,1024,768]{2,1,0:T(8,128)(2,1)} %param.26), kind=kOutput, calls=%fused_computation.27 | convolution fusion | flops 2420244480 | bytes 8650752 | tf_op jit(solution)/shard_map/dot_general | solution.py:165
  266.0 5.2 %all-to-all-start.5 = ((bf16[16,48,1024]{2,1,0:T(8,128)(2,1)}), bf16[16,48,1024]{2,1,0:T(8,128)(2,1)S(1)}, u32[]{:S(2)}, u32[]{:S(2)}) async-start(bf16[16,48,1024]{2,1,0:T(8,128)(2,1)} %bitcast.124), calls=%async_computation.5 | async-start | bytes 3145728 | tf_op jit(solution)/shard_map/all_to_all | solution.py:169
  271.4 31.7 %all-to-all-done.5 = bf16[16,48,1024]{2,1,0:T(8,128)(2,1)S(1)} async-done(((bf16[16,48,1024]{2,1,0:T(8,128)(2,1)}), bf16[16,48,1024]{2,1,0:T(8,128)(2,1)S(1)}, u32[]{:S(2)}, u32[]{:S(2)}) %all-to-all-start.5) | async-done | bytes 1572896 | tf_op jit(solution)/shard_map/all_to_all | solution.py:169
  303.1 2.8 gather_fusion.5
  (139 shorter events, 44.1 us)
Async XLA Ops:
  0.0 259.4 %copy-start = (bf16[1,768,1024]{2,1,0:T(8,128)(2,1)S(1)}, bf16[1,768,1024]{2,1,0:T(8,128)(2,1)}, u32[]{:S(2)}) copy-start(bf16[1,768,1024]{2,1,0:T(8,128)(2,1)} %param.27) | copy-start | bytes 4718596
  0.0 6.1 %copy-start.1 = (bf16[64,2048]{1,0:T(8,128)(2,1)S(1)}, bf16[64,2048]{1,0:T(8,128)(2,1)}, u32[]{:S(2)}) copy-start(bf16[64,2048]{1,0:T(8,128)(2,1)} %param.14) | copy-start | bytes 786436
  79.1 3.8 %copy-start.11 = (bf16[512,256]{1,0:T(8,128)(2,1)S(1)}, bf16[512,256]{1,0:T(8,128)(2,1)}, u32[]{:S(2)}) copy-start(bf16[512,256]{1,0:T(8,128)(2,1)} %param.15) | copy-start | bytes 786436
  88.6 7.0 %copy-start.2 = (f32[5120,512]{0,1:T(8,128)S(1)}, f32[5120,512]{0,1:T(8,128)}, u32[]{:S(2)}) copy-start(f32[5120,512]{0,1:T(8,128)} %get-tuple-element.12) | copy-start | bytes 31457284
  95.5 3.3 %copy-start.3 = (bf16[5120,128]{1,0:T(8,128)(2,1)S(1)}, bf16[5120,128]{1,0:T(8,128)(2,1)}, u32[]{:S(2)}) copy-start(bf16[5120,128]{1,0:T(8,128)(2,1)} %reshape.314) | copy-start | bytes 3932164
  95.6 3.3 %copy-start.12 = (bf16[512,256]{1,0:T(8,128)(2,1)S(1)}, bf16[512,256]{1,0:T(8,128)(2,1)}, u32[]{:S(2)}) copy-start(bf16[512,256]{1,0:T(8,128)(2,1)} %param.15) | copy-start | bytes 786436
  100.4 2.3 copy-start.13
  109.2 3.7 %copy-start.8 = (f32[16,40,8]{2,1,0:T(8,128)S(1)}, f32[16,40,8]{2,1,0:T(8,128)}, u32[]{:S(2)}) copy-start(f32[16,40,8]{2,1,0:T(8,128)} %concatenate.73) | copy-start | bytes 61444
  109.5 21.3 %copy-start.4 = (bf16[16,40,1024]{2,1,0:T(8,128)(2,1)S(1)}, bf16[16,40,1024]{2,1,0:T(8,128)(2,1)}, u32[]{:S(2)}) copy-start(bf16[16,40,1024]{2,1,0:T(8,128)(2,1)} %concatenate.77) | copy-start | bytes 3932164
  115.3 12.0 %all-to-all-start.1 = ((f32[16,1,640]{2,1,0:T(1,128)}), f32[16,1,640]{2,1,0:T(1,128)}, u32[]{:S(2)}, u32[]{:S(2)}) async-start(f32[16,1,640]{2,1,0:T(1,128)} %reshape.403), calls=%async_computation.1 | async-start | bytes 81920 | tf_op jit(solution)/shard_map/all_to_all | solution.py:105
  127.3 10.2 %all-to-all-start.3 = ((f32[16,1,640]{2,1,0:T(1,128)}), f32[16,1,640]{2,1,0:T(1,128)S(1)}, u32[]{:S(2)}, u32[]{:S(2)}) async-start(f32[16,1,640]{2,1,0:T(1,128)} %reshape.405), calls=%async_computation.3 | async-start | bytes 81920 | tf_op jit(solution)/shard_map/all_to_all | solution.py:108
  133.9 8.0 %copy-start.17 = (s32[64,8]{0,1:T(8,128)S(1)}, s32[64,8]{0,1:T(8,128)}, u32[]{:S(2)}) copy-start(s32[64,8]{0,1:T(8,128)} %param.23) | copy-start | bytes 6148
  133.9 12.7 %copy-start.15 = (bf16[64,256]{1,0:T(8,128)(2,1)S(1)}, bf16[64,256]{1,0:T(8,128)(2,1)}, u32[]{:S(2)}) copy-start(bf16[64,256]{1,0:T(8,128)(2,1)} %param.17) | copy-start | bytes 98308
  137.4 54.6 %all-to-all-start.2 = ((bf16[16,40,2048]{2,1,0:T(8,128)(2,1)}), bf16[16,40,2048]{2,1,0:T(8,128)(2,1)}, u32[]{:S(2)}, u32[]{:S(2)}) async-start(bf16[16,40,2048]{2,1,0:T(8,128)(2,1)} %pad_maximum_fusion), calls=%async_computation.2 | async-start | bytes 5242880 | tf_op jit(solution)/shard_map/all_to_all | solution.py:115
  141.9 6.9 %copy-start.16 = (bf16[64,256]{1,0:T(8,128)(2,1)S(1)}, bf16[64,256]{1,0:T(8,128)(2,1)}, u32[]{:S(2)}) copy-start(bf16[64,256]{1,0:T(8,128)(2,1)} %param.18) | copy-start | bytes 98308
  146.9 8.1 %copy-start.9 = (f32[64,8]{1,0:T(8,128)}, f32[64,8]{1,0:T(8,128)S(1)}, u32[]{:S(2)}) copy-start(f32[64,8]{1,0:T(8,128)S(1)} %concatenate.70) | copy-start | bytes 6148
  148.0 7.0 %copy-start.10 = (f32[64,8]{1,0:T(8,128)}, f32[64,8]{1,0:T(8,128)S(1)}, u32[]{:S(2)}) copy-start(f32[64,8]{1,0:T(8,128)S(1)} %concatenate.71) | copy-start | bytes 6148
  199.3 3.3 %copy-start.5 = (bf16[2048,1024]{1,0:T(8,128)(2,1)S(1)}, bf16[2048,1024]{1,0:T(8,128)(2,1)}, u32[]{:S(2)}) copy-start(bf16[2048,1024]{1,0:T(8,128)(2,1)} %param.21) | copy-start | bytes 12582916
  199.3 3.3 %copy-start.14 = (bf16[64,1024]{1,0:T(8,128)(2,1)S(1)}, bf16[64,1024]{1,0:T(8,128)(2,1)}, u32[]{:S(2)}) copy-start(bf16[64,1024]{1,0:T(8,128)(2,1)} %param.20) | copy-start | bytes 393220
  202.6 1.7 copy-start.19
  207.4 49.2 %copy-start.20 = (bf16[1,1024,768]{2,1,0:T(8,128)(2,1)S(1)}, bf16[1,1024,768]{2,1,0:T(8,128)(2,1)}, u32[]{:S(2)}) copy-start(bf16[1,1024,768]{2,1,0:T(8,128)(2,1)} %param.25) | copy-start | bytes 4718596
  266.0 5.2 %copy-start.18 = (f32[64,8]{0,1:T(8,128)S(1)}, f32[64,8]{0,1:T(8,128)}, u32[]{:S(2)}) copy-start(f32[64,8]{0,1:T(8,128)} %param.24) | copy-start | bytes 6148
  266.0 37.0 %all-to-all-start.5 = ((bf16[16,48,1024]{2,1,0:T(8,128)(2,1)}), bf16[16,48,1024]{2,1,0:T(8,128)(2,1)S(1)}, u32[]{:S(2)}, u32[]{:S(2)}) async-start(bf16[16,48,1024]{2,1,0:T(8,128)(2,1)} %bitcast.124), calls=%async_computation.5 | async-start | bytes 3145728 | tf_op jit(solution)/shard_map/all_to_all | solution.py:169
  303.1 4.4 %copy-start.7 = (f32[64,1024]{1,0:T(8,128)S(1)}, f32[64,1024]{1,0:T(8,128)}, u32[]{:S(2)}) copy-start(f32[64,1024]{1,0:T(8,128)} %copy-done.6) | copy-start | bytes 786436
  (1 other events, 0.7 us)
where the time goes:
time: 313 us; the launch traced here: 308 us
  blocking collectives  115 us (37%)
  waiting for transfers between devices  74.1 us (24%)
  local copies, waits for them, and re-layouts  47.4 us (15%)
  matrix products  29.4 us (9%)
  other arithmetic  23.5 us (8%)
  starting transfers between devices  18.4 us (6%)
    all_to_all x1, blocking collectives, body(): lax.all_to_all(outgoing, 'blk', split_axis=0, concat_axis=0, tiled=True)  65.6 us
    all_to_all x1, blocking collectives, body(): lax.all_to_all(dispatched, 'blk', split_axis=0, concat_axis=0, tiled=True)  49.1 us
    all_to_all x1, waiting for transfers between devices, body(): lax.all_to_all(far_out.astype(jnp.bfloat16).reshape(senders, items, row_w...  35.5 us
    all_to_all x1, waiting for transfers between devices, body(): lax.all_to_all(expert_out, 'blk', split_axis=0, concat_axis=0, tiled=True)  31.7 us
    reduce_sum x4, other arithmetic, partials(): totals.append(jnp.sum(weights, axis=1).reshape(-1, queries_per_cluster))  8.28 us
    dot_general x4, matrix products, partials(): lax.dot_general(group_queries, group_keys, (((1,), (1,)), ((), ())), pref...  7.43 us
    gather x1, local copies, waits for them, and re-layouts, body(): back_out.reshape(-1, QUERY_HEADS * HEAD_SIZE)[owner_slots]  7.29 us
    dot_general x4, matrix products, partials(): jnp.dot(weights.astype(jnp.bfloat16), group_values, preferred_element_typ...  7.03 us
  transfers between devices with their start and end apart: 4, of which 4 were waited for; matrix products, arithmetic and copies ran while one was open for 7% of the time, Pallas kernels for 0%

commit v1 on v0

--- a/solution.py
+++ b/solution.py
@@ -1,6 +1,10 @@
+import functools
+
 import jax
 import jax.numpy as jnp
 from jax import lax
+from jax.experimental import pallas as pl
+from jax.experimental.pallas import tpu as pltpu
 from jax.sharding import PartitionSpec as P
 
 QUERY_HEADS = 16
@@ -175,6 +179,554 @@
     return (hidden_state + mixture).astype(jnp.bfloat16)
 
 
+LANES = 128
+LOW_PART = 64
+MESH = pl.DeviceIdType.MESH
+LOG2_E = 1.4426950408889634
+
+
+def place_of(index):
+    return lax.div(index, 4), lax.rem(lax.div(index, 2), 2), lax.rem(index, 2)
+
+
+def index_of(z, x, c):
+    return (z * 2 + x) * 2 + c
+
+
+def nth_plane(k, z, planes):
+    low = jnp.minimum(z, planes - 1 - z)
+    near = k <= 2 * low
+    far = jnp.where(near, lax.div(k + 1, 2), k - low)
+    up = jnp.where(near, lax.rem(k, 2), (z < planes - 1 - z).astype(jnp.int32))
+    return z + far * (2 * up - 1)
+
+
+class Gather:
+    def __init__(self, planes, bufs, send_sem, recv_sem):
+        self.planes, self.bufs, self.send_sem, self.recv_sem = planes, bufs, send_sem, recv_sem
+        self.me = lax.axis_index("blk")
+        self.z, self.x, self.c = place_of(self.me)
+
+    def copy(self, part, way, block, target):
+        return pltpu.make_async_remote_copy(
+            src_ref=self.bufs[part].at[block],
+            dst_ref=self.bufs[part].at[block],
+            send_sem=self.send_sem.at[part, way, block],
+            recv_sem=self.recv_sem.at[part, block],
+            device_id={"blk": target},
+            device_id_type=MESH,
+        )
+
+    def arrive(self, part, block):
+        self.copy(part, 3, block, index_of(self.z, self.x, 1 - self.c)).wait_recv()
+
+    def column_ways(self, plane):
+        up = jnp.logical_and(plane <= self.z, self.z < self.planes - 1)
+        down = jnp.logical_and(plane >= self.z, self.z > 0)
+        return up, down
+
+    def pass_column(self, part, plane):
+        z, x, c = self.z, self.x, self.c
+        block = index_of(plane, x, c)
+        up, down = self.column_ways(plane)
+
+        @pl.when(up)
+        def _():
+            self.copy(part, 0, block, index_of(z + 1, x, c)).start()
+
+        @pl.when(down)
+        def _():
+            self.copy(part, 1, block, index_of(z - 1, x, c)).start()
+
+        self.copy(part, 2, block, index_of(z, 1 - x, c)).start()
+        self.copy(part, 3, block, index_of(z, x, 1 - c)).start()
+
+    def take_column(self, k):
+        plane = nth_plane(k, self.z, self.planes)
+        for part in range(len(self.bufs)):
+
+            @pl.when(k > 0)
+            def _():
+                self.arrive(part, index_of(plane, self.x, self.c))
+
+            self.pass_column(part, plane)
+
+    def take_across(self, k):
+        plane = nth_plane(k, self.z, self.planes)
+        block = index_of(plane, 1 - self.x, self.c)
+        for part in range(len(self.bufs)):
+            self.arrive(part, block)
+            self.copy(part, 3, block, index_of(self.z, self.x, 1 - self.c)).start()
+
+    def take_partner(self, k, x):
+        plane = nth_plane(k, self.z, self.planes)
+        for part in range(len(self.bufs)):
+            self.arrive(part, index_of(plane, x, 1 - self.c))
+
+    def finish(self):
+        z, x, c = self.z, self.x, self.c
+
+        @pl.loop(0, self.planes)
+        def _(plane):
+            block = index_of(plane, x, c)
+            across = index_of(plane, 1 - x, c)
+            up, down = self.column_ways(plane)
+            for part in range(len(self.bufs)):
+
+                @pl.when(up)
+                def _():
+                    self.copy(part, 0, block, index_of(z + 1, x, c)).wait_send()
+
+                @pl.when(down)
+                def _():
+                    self.copy(part, 1, block, index_of(z - 1, x, c)).wait_send()
+
+                self.copy(part, 2, block, index_of(z, 1 - x, c)).wait_send()
+                self.copy(part, 3, block, index_of(z, x, 1 - c)).wait_send()
+                self.copy(part, 3, across, index_of(z, x, 1 - c)).wait_send()
+
+
+def greet(planes, z, x, c):
+    barrier = pltpu.get_barrier_semaphore()
+    for target in (index_of(z, 1 - x, c), index_of(z, x, 1 - c)):
+        pl.semaphore_signal(barrier, inc=1, device_id={"blk": target}, device_id_type=MESH)
+
+    @pl.loop(0, planes)
+    def _(plane):
+        @pl.when(plane != z)
+        def _():
+            pl.semaphore_signal(
+                barrier, inc=1, device_id={"blk": index_of(plane, x, c)}, device_id_type=MESH
+            )
+
+    pl.semaphore_wait(barrier, planes + 1)
+
+
+def attention_kernel(
+    planes,
+    q_ref,
+    k_any,
+    v_any,
+    new_k_ref,
+    new_v_ref,
+    ids_ref,
+    residual_ref,
+    weight_any,
+    gain_ref,
+    experts_ref,
+    gates_ref,
+    hidden_ref,
+    rows_ref,
+    k_buf,
+    v_buf,
+    weight_buf,
+    q_buf,
+    att_buf,
+    max_buf,
+    sum_buf,
+    acc_buf,
+    local_sem,
+    send_sem,
+    recv_sem,
+):
+    gather = Gather(planes, (k_buf, v_buf), send_sem, recv_sem)
+    me, z, x, c = gather.me, gather.z, gather.x, gather.c
+    own = [
+        pltpu.make_async_copy(k_any, k_buf.at[me], local_sem.at[0]),
+        pltpu.make_async_copy(v_any, v_buf.at[me], local_sem.at[1]),
+    ]
+    weights_in = pltpu.make_async_copy(weight_any, weight_buf, local_sem.at[2])
+    for copy in own:
+        copy.start()
+    greet(planes, z, x, c)
+    for copy in own:
+        copy.wait()
+    gather.take_column(jnp.int32(0))
+    weights_in.start()
+
+    tokens = q_ref.shape[0]
+    chunks, chunk_rows, _ = q_buf.shape
+    heads = chunk_rows // tokens
+    chunks_per_group = chunks // KEY_VALUE_HEADS
+    factor = HEAD_SIZE ** (-0.5) * LOG2_E
+
+    for chunk in range(chunks):
+        group = chunk // chunks_per_group
+        lanes = slice(group * HEAD_SIZE, (group + 1) * HEAD_SIZE)
+        for head in range(heads):
+            at = (chunk * heads + head) * HEAD_SIZE
+            q_buf[chunk, head * tokens : (head + 1) * tokens, :] = q_ref[:, at : at + HEAD_SIZE]
+        scores = lax.dot_general(
+            q_buf[chunk],
+            new_k_ref[:, lanes],
+            (((1,), (1,)), ((), ())),
+            preferred_element_type=jnp.float32,
+        )
+        row = lax.rem(lax.broadcasted_iota(jnp.int32, scores.shape, 0), tokens)
+        key = lax.broadcasted_iota(jnp.int32, scores.shape, 1)
+        scores = jnp.where(key <= row, scores, -jnp.inf)
+        top = jnp.max(scores, axis=1, keepdims=True)
+        weights = jnp.exp2((scores - top) * factor)
+        max_buf[chunk] = top
+        sum_buf[chunk] = jnp.sum(weights, axis=1, keepdims=True)
+        acc_buf[chunk] = jnp.dot(
+            weights.astype(jnp.bfloat16), new_v_ref[:, lanes], preferred_element_type=jnp.float32
+        )
+
+    @pl.loop(0, 4 * (planes + 1))
+    def _(step):
+        k, kind = lax.div(step, 4), lax.rem(step, 4)
+        late = lax.div(kind, 2)
+        valid = jnp.logical_or(
+            jnp.logical_and(late == 0, k < planes), jnp.logical_and(late == 1, k > 0)
+        )
+
+        @pl.when(valid)
+        def _():
+            place = k - late
+            plane = nth_plane(place, z, planes)
+
+            @pl.when(jnp.logical_and(kind == 0, k > 0))
+            def _():
+                gather.take_column(k)
+
+            @pl.when(kind == 1)
+            def _():
+                gather.take_partner(place, x)
+
+            @pl.when(kind == 2)
+            def _():
+                gather.take_across(place)
+
+            @pl.when(kind == 3)
+            def _():
+                gather.take_partner(place, 1 - x)
+
+            other_core = lax.rem(kind, 2)
+            block = index_of(
+                plane,
+                x + late * (1 - 2 * x),
+                c + other_core * (1 - 2 * c),
+            )
+            named = jnp.sum(
+                jnp.where(ids_ref[...] == block, jnp.float32(1), jnp.float32(0)),
+                axis=1,
+                keepdims=True,
+            )
+            named = jnp.concatenate([named] * heads, axis=0) > 0.5
+            for chunk in range(chunks):
+                group = chunk // chunks_per_group
+                lanes = slice(group * HEAD_SIZE, (group + 1) * HEAD_SIZE)
+                scores = lax.dot_general(
+                    q_buf[chunk],
+                    k_buf[block, :, lanes],
+                    (((1,), (1,)), ((), ())),
+                    preferred_element_type=jnp.float32,
+                )
+                before = max_buf[chunk]
+                top = jnp.maximum(before, jnp.max(scores, axis=1, keepdims=True))
+                weights = jnp.exp2((scores - top) * factor)
+                scale = jnp.where(named, jnp.exp2((before - top) * factor), 1.0)
+                total = jnp.sum(weights, axis=1, keepdims=True)
+                mixed = jnp.dot(
+                    weights.astype(jnp.bfloat16),
+                    v_buf[block, :, lanes],
+                    preferred_element_type=jnp.float32,
+                )
+                max_buf[chunk] = jnp.where(named, top, before)
+                sum_buf[chunk] = sum_buf[chunk] * scale + jnp.where(named, total, 0.0)
+                acc_buf[chunk] = acc_buf[chunk] * scale + jnp.where(named, mixed, 0.0)
+
+    for chunk in range(chunks):
+        attention = (acc_buf[chunk] / sum_buf[chunk]).astype(jnp.bfloat16)
+        for head in range(heads):
+            at = (chunk * heads + head) * HEAD_SIZE
+            att_buf[:, at : at + HEAD_SIZE] = attention[head * tokens : (head + 1) * tokens]
+    weights_in.wait()
+    hidden = residual_ref[...].astype(jnp.float32) + jnp.dot(
+        att_buf[...], weight_buf[...], preferred_element_type=jnp.float32
+    )
+    hidden_ref[...] = hidden
+    width = hidden.shape[1]
+    normed = (
+        hidden
+        * lax.rsqrt(jnp.mean(hidden * hidden, axis=-1, keepdims=True) + NORM_EPSILON)
+        * gain_ref[...]
+    )
+    rows_ref[:, :width] = normed.astype(jnp.bfloat16)
+    gates = gates_ref[...]
+    mixing = gates / jnp.sum(gates, axis=1, keepdims=True)
+    lane = lax.broadcasted_iota(jnp.int32, (tokens, LANES), 1)
+    spread = jnp.zeros((tokens, LANES), jnp.float32)
+    for choice in range(TOPE):
+        expert = experts_ref[:, choice : choice + 1]
+        hit = jnp.logical_or(lane == expert, lane == expert + LOW_PART)
+        spread += jnp.where(hit, mixing[:, choice : choice + 1], 0.0)
+    high = spread.astype(jnp.bfloat16).astype(jnp.float32)
+    rows_ref[:, width:] = jnp.where(lane < LOW_PART, high, spread - high).astype(jnp.bfloat16)
+    gather.finish()
+
+
+def expert_kernel(
+    planes,
+    rows_any,
+    hidden_ref,
+    gate_any,
+    up_any,
+    down_any,
+    out_ref,
+    row_buf,
+    gate_buf,
+    up_buf,
+    down_buf,
+    part_buf,
+    core_out,
+    core_in,
+    across_out,
+    across_in,
+    plane_out,
+    plane_in,
+    local_sem,
+    send_sem,
+    recv_sem,
+    back_send,
+    back_recv,
+):
+    gather = Gather(planes, (row_buf,), send_sem, recv_sem)
+    me, z, x, c = gather.me, gather.z, gather.x, gather.c
+    tokens, width = hidden_ref.shape
+    own = pltpu.make_async_copy(rows_any, row_buf.at[me], local_sem.at[0])
+    own.start()
+    weights_in = [
+        pltpu.make_async_copy(source.at[0], target, local_sem.at[1 + i])
+        for i, (source, target) in enumerate(
+            ((gate_any, gate_buf), (up_any, up_buf), (down_any, down_buf))
+        )
+    ]
+    greet(planes, z, x, c)
+    own.wait()
+    gather.take_column(jnp.int32(0))
+    for copy in weights_in:
+        copy.start()
+    for copy in weights_in:
+        copy.wait()
+
+    def to_core(plane):
+        return pltpu.make_async_remote_copy(
+            src_ref=core_out.at[plane],
+            dst_ref=core_in.at[plane],
+            send_sem=back_send.at[0, plane],
+            recv_sem=back_recv.at[0, plane],
+            device_id={"blk": index_of(z, x, 1 - c)},
+            device_id_type=MESH,
+        )
+
+    def to_across(plane):
+        return pltpu.make_async_remote_copy(
+            src_ref=across_out.at[plane],
+            dst_ref=across_in.at[plane],
+            send_sem=back_send.at[1, plane],
+            recv_sem=back_recv.at[1, plane],
+            device_id={"blk": index_of(z, 1 - x, c)},
+            device_id_type=MESH,
+        )
+
+    def to_plane(plane, sender):
+        return pltpu.make_async_remote_copy(
+            src_ref=plane_out.at[plane],
+            dst_ref=plane_in.at[sender],
+            send_sem=back_send.at[2, plane],
+            recv_sem=back_recv.at[2, sender],
+            device_id={"blk": index_of(plane, x, c)},
+            device_id_type=MESH,
+        )
+
+    @pl.loop(1, planes + 4)
+    def _(k):
+        @pl.when(k < planes)
+        def _():
+            gather.take_column(k)
+
+        @pl.when(jnp.logical_and(k >= 1, k <= planes))
+        def _():
+            place = k - 1
+            plane = nth_plane(place, z, planes)
+            gather.take_across(place)
+            gather.take_partner(place, x)
+            gather.take_partner(place, 1 - x)
+            rows = row_buf[pl.ds(plane * 4, 4)].reshape(4 * tokens, width + LANES)
+            shares = rows[:, width:].astype(jnp.float32)
+            lane = lax.broadcasted_iota(jnp.int32, shares.shape, 1)
+            hit = jnp.logical_or(lane == me, lane == me + LOW_PART)
+            share = jnp.sum(jnp.where(hit, shares, 0.0), axis=1, keepdims=True)
+            rows = rows[:, :width]
+            gate_part = jnp.dot(rows, gate_buf[...], preferred_element_type=jnp.float32)
+            up_part = jnp.dot(rows, up_buf[...], preferred_element_type=jnp.float32)
+            inner = (gate_part / (1.0 + jnp.exp(-gate_part)) * up_part).astype(jnp.bfloat16)
+            result = share * jnp.dot(inner, down_buf[...], preferred_element_type=jnp.float32)
+            part_buf[pl.ds(plane * 4, 4)] = result.reshape(4, tokens, width)
+            for there in range(2):
+                core_out[plane, there] = part_buf[index_of(plane, there, 1 - c)].astype(
+                    jnp.bfloat16
+                )
+            to_core(plane).start()
+
+        @pl.when(jnp.logical_and(k >= 2, k <= planes + 1))
+        def _():
+            plane = nth_plane(k - 2, z, planes)
+            to_core(plane).wait_recv()
+            across_out[plane] = (
+                part_buf[index_of(plane, 1 - x, c)]
+                + core_in[plane, 1 - x].astype(jnp.float32)
+            ).astype(jnp.bfloat16)
+            to_across(plane).start()
+
+        @pl.when(k >= 3)
+        def _():
+            @pl.when(k <= planes + 2)
+            def _():
+                plane = nth_plane(k - 3, z, planes)
+                to_across(plane).wait_recv()
+                total = (
+                    part_buf[index_of(plane, x, c)]
+                    + core_in[plane, x].astype(jnp.float32)
+                    + across_in[plane].astype(jnp.float32)
+                )
+                part_buf[index_of(plane, x, c)] = total
+
+                @pl.when(plane != z)
+                def _():
+                    plane_out[plane] = total.astype(jnp.bfloat16)
+                    to_plane(plane, z).start()
+
+    out = hidden_ref[...] + part_buf[me]
+    part_buf[me] = out
+
+    @pl.loop(0, planes)
+    def _(plane):
+        @pl.when(plane != z)
+        def _():
+            to_plane(z, plane).wait_recv()
+            part_buf[me] += plane_in[plane].astype(jnp.float32)
+
+    out_ref[...] = part_buf[me].astype(jnp.bfloat16)
+
+    @pl.loop(0, planes)
+    def _(plane):
+        to_core(plane).wait_send()
+        to_across(plane).wait_send()
+
+        @pl.when(plane != z)
+        def _():
+            to_plane(plane, z).wait_send()
+
+    gather.finish()
+
+
+def gathered(
+    queries,
+    rotated_cache_keys,
+    stored_cache_values,
+    segment_new_keys,
+    segment_new_values,
+    block_ids,
+    residual_in,
+    out_weight,
+    norm_gain,
+    expert_ids,
+    gate_scores,
+    w_gate,
+    w_up,
+    w_down,
+):
+    parties = lax.axis_size("blk")
+    planes = parties // 4
+    tokens, width = residual_in.shape
+    bf16, f32 = jnp.bfloat16, jnp.float32
+    chunks = 4
+    chunk_rows = tokens * QUERY_HEADS // chunks
+    inside = pl.BlockSpec(memory_space=pltpu.VMEM)
+    outside = pl.BlockSpec(memory_space=pl.ANY)
+    hidden, rows = pl.pallas_call(
+        functools.partial(attention_kernel, planes),
+        out_shape=(
+            jax.ShapeDtypeStruct((tokens, width), f32),
+            jax.ShapeDtypeStruct((tokens, width + LANES), bf16),
+        ),
+        in_specs=[inside, outside, outside] + [inside] * 4 + [outside] + [inside] * 3,
+        out_specs=(inside, inside),
+        scratch_shapes=[
+            pltpu.VMEM((parties,) + rotated_cache_keys.shape, bf16),
+            pltpu.VMEM((parties,) + stored_cache_values.shape, bf16),
+            pltpu.VMEM(out_weight.shape, bf16),
+            pltpu.VMEM((chunks, chunk_rows, HEAD_SIZE), bf16),
+            pltpu.VMEM((tokens, QUERY_HEADS * HEAD_SIZE), bf16),
+            pltpu.VMEM((chunks, chunk_rows, 1), f32),
+            pltpu.VMEM((chunks, chunk_rows, 1), f32),
+            pltpu.VMEM((chunks, chunk_rows, HEAD_SIZE), f32),
+            pltpu.SemaphoreType.DMA((3,)),
+            pltpu.SemaphoreType.DMA((2, 4, parties)),
+            pltpu.SemaphoreType.DMA((2, parties)),
+        ],
+        compiler_params=pltpu.CompilerParams(
+            collective_id=0, has_side_effects=True, vmem_limit_bytes=48 << 20
+        ),
+        name="attention",
+    )(
+        queries,
+        rotated_cache_keys,
+        stored_cache_values,
+        segment_new_keys,
+        segment_new_values,
+        block_ids,
+        residual_in,
+        out_weight,
+        norm_gain[None, :],
+        expert_ids,
+        gate_scores,
+    )
+    back = (planes, tokens, width)
+    return pl.pallas_call(
+        functools.partial(expert_kernel, planes),
+        out_shape=jax.ShapeDtypeStruct((tokens, width), bf16),
+        in_specs=[outside, inside, outside, outside, outside],
+        out_specs=inside,
+        scratch_shapes=[
+            pltpu.VMEM((parties, tokens, width + LANES), bf16),
+            pltpu.VMEM(w_gate.shape[1:], bf16),
+            pltpu.VMEM(w_up.shape[1:], bf16),
+            pltpu.VMEM(w_down.shape[1:], bf16),
+            pltpu.VMEM((parties, tokens, width), f32),
+            pltpu.VMEM((planes, 2, tokens, width), bf16),
+            pltpu.VMEM((planes, 2, tokens, width), bf16),
+            pltpu.VMEM(back, bf16),
+            pltpu.VMEM(back, bf16),
+            pltpu.VMEM(back, bf16),
+            pltpu.VMEM(back, bf16),
+            pltpu.SemaphoreType.DMA((4,)),
+            pltpu.SemaphoreType.DMA((1, 4, parties)),
+            pltpu.SemaphoreType.DMA((1, parties)),
+            pltpu.SemaphoreType.DMA((3, planes)),
+            pltpu.SemaphoreType.DMA((3, planes)),
+        ],
+        compiler_params=pltpu.CompilerParams(
+            collective_id=1, has_side_effects=True, vmem_limit_bytes=48 << 20
+        ),
+        name="experts",
+    )(rows, hidden, w_gate, w_up, w_down)
+
+
+GATHER_LIMIT_BYTES = 24 << 20
+
+
+def layer(*operands):
+    parties = lax.axis_size("blk")
+    keys, values = operands[1], operands[2]
+    cache_bytes = parties * (keys.size + values.size) * keys.dtype.itemsize
+    fits = cache_bytes <= GATHER_LIMIT_BYTES and parties % 4 == 0 and parties <= LOW_PART
+    return gathered(*operands) if fits else body(*operands)
+
+
 def solution(mesh):
     placed = (
         P(("groups", "blk"), None),
@@ -193,5 +745,5 @@
         P("blk", None, None),
     )
     return jax.shard_map(
-        body, mesh=mesh, in_specs=placed, out_specs=P(("groups", "blk"), None), check_vma=False
-    )
+        layer, mesh=mesh, in_specs=placed, out_specs=P(("groups", "blk"), None), check_vma=False
+    )

time: 313 us -> 120 us (0.38); the launches traced: 308 us -> 119 us
  blocking collectives: 115 us -> 0 us
  Pallas kernels: 0 us -> 108 us
  waiting for transfers between devices: 74.1 us -> 0 us
  local copies, waits for them, and re-layouts: 47.4 us -> 11.1 us
  matrix products: 29.4 us -> 0 us
  other arithmetic: 23.5 us -> 0 us
  starting transfers between devices: 18.4 us -> 0 us
    all_to_all x2 -> x0, blocking collectives: 115 us -> none  [the longest x1 65.6 us: body(): lax.all_to_all(outgoing, 'blk', split_axis=0, concat_axis=0, tiled=True)]
    pallas_call x0 -> x2, Pallas kernels: none -> 108 us  [the longest x1 60.8 us: gathered(): pl.pallas_call(functools.partial(attention_kernel, planes), out_shape=(ja...]
    all_to_all x4 -> x0, waiting for transfers between devices: 74.1 us -> none  [the longest x1 35.5 us: body(): lax.all_to_all(far_out.astype(jnp.bfloat16).reshape(senders, items, row_w...]
    dot_general x13 -> x0, matrix products: 29.4 us -> none  [the longest x4 7.43 us: partials(): lax.dot_general(group_queries, group_keys, (((1,), (1,)), ((), ())), pref...]
    gather x6 -> x0, local copies, waits for them, and re-layouts: 19 us -> none  [the longest x1 7.29 us: body(): back_out.reshape(-1, QUERY_HEADS * HEAD_SIZE)[owner_slots]]
    all_to_all x4 -> x0, starting transfers between devices: 18.4 us -> none  [the longest x1 5.22 us: body(): lax.all_to_all(far_max.reshape(senders, items, QUERY_HEADS), 'blk', split...]
    concatenate x14 -> x0, local copies, waits for them, and re-layouts: 11 us -> none  [the longest x2 4.8 us: partials(): jnp.concatenate(outputs, axis=1)]
    reduce_sum x8 -> x0, other arithmetic: 8.61 us -> none  [the longest x4 8.28 us: partials(): totals.append(jnp.sum(weights, axis=1).reshape(-1, queries_per_cluster))]
  transfers between devices with their start and end apart: 4 -> 0, of which waited for: 4 -> 0; matrix products, arithmetic and copies ran while one was open for 7% -> 0% of each run, Pallas kernels for 0% -> 0%
where the time goes in v1:
time: 120 us; the launch traced here: 119 us
  Pallas kernels  108 us (90%)
  local copies, waits for them, and re-layouts  11.1 us (9%)
    pallas_call x1, Pallas kernels, gathered(): pl.pallas_call(functools.partial(attention_kernel, planes), out_shape=(ja...  60.8 us
    pallas_call x1, Pallas kernels, gathered(): pl.pallas_call(functools.partial(expert_kernel, planes), out_shape=jax.Sh...  47.2 us
    unnamed x26, local copies, waits for them, and re-layouts  11.1 us

profile of v1, /device:TPU:0, one launch (start us, length us, event | category | flops | bytes accessed | tf_op | source)
XLA Modules:
  0.0 119.1 jit_solution(9919456418545140811)
XLA Ops:
  0.0 0.8 copy.15.ids_ref
  0.8 0.8 copy.16.experts_ref
  1.5 0.8 copy.17.gates_ref
  2.3 0.0 copy-start
  2.3 2.2 %copy-done = bf16[2048,1024]{1,0:T(8,128)(2,1)S(1)} copy-done((bf16[2048,1024]{1,0:T(8,128)(2,1)S(1)}, bf16[2048,1024]{1,0:T(8,128)(2,1)}, u32[]{:S(2)}) %copy-start) | copy-done | bytes 4194328
  4.5 0.0 copy-start.4
  4.5 0.9 copy-done.4
  5.4 0.0 copy-start.5
  5.5 0.9 copy-done.5
  6.4 0.0 copy-start.6
  6.4 0.9 copy-done.6
  7.4 0.0 copy-start.7
  7.4 0.9 copy-done.7
  8.3 0.0 copy-start.8
  8.3 0.8 copy-done.8
  9.0 0.8 copy-done.9
  9.8 0.0 copy-start.10
  9.8 0.7 copy-done.10
  10.5 60.8 %attention.1 = (f32[64,1024]{1,0:T(8,128)S(1)}, bf16[64,1152]{1,0:T(8,128)(2,1)S(1)}) custom-call(bf16[64,2048]{1,0:T(8,128)(2,1)S(1)} %copy-done.4, bf16[512,256]{1,0:T(8,128)(2,1)S(1)} %copy-done.5, bf16[512,256]{1,0:T(8,128)(2,1)S(1)} %copy-done.6, bf16[64,256]{1,0:T(8,128)(2,1)S(1)} %copy-done.8, bf16[64,256]{1,0:T(8,128)(2,1)S(1)} %copy-done.9, ...), custom_call_target="tpu_custom_call" | custom-call | tf_op jit(solution)/shard_map/attention/pallas_call | solution.py:650
  71.3 0.0 copy-done.1
  71.3 0.0 copy-done.2
  71.3 0.0 copy-done.3
  71.3 47.2 %experts.1 = bf16[64,1024]{1,0:T(8,128)(2,1)S(1)} custom-call(bf16[64,1152]{1,0:T(8,128)(2,1)S(1)} %get-tuple-element.7.rows_any, f32[64,1024]{1,0:T(8,128)S(1)} %get-tuple-element.8.hidden_ref, bf16[1,1024,768]{2,1,0:T(8,128)(2,1)S(1)} %copy-done.1, bf16[1,1024,768]{2,1,0:T(8,128)(2,1)S(1)} %copy-done.2, bf16[1,768,1024]{2,1,0:T(8,128)(2,1)S(1)} %copy-done.3), custom_call_target="tpu_custom_call" | custom-call | tf_op jit(solution)/shard_map/experts/pallas_call | solution.py:689
  118.5 0.7 copy.19
  (4 shorter events, 0.0 us)
Async XLA Ops:
  2.3 2.2 %copy-start = (bf16[2048,1024]{1,0:T(8,128)(2,1)S(1)}, bf16[2048,1024]{1,0:T(8,128)(2,1)}, u32[]{:S(2)}) copy-start(bf16[2048,1024]{1,0:T(8,128)(2,1)} %weight_any.1) | copy-start | bytes 12582916
  4.5 0.9 copy-start.4
  5.4 0.9 copy-start.5
  6.4 0.9 copy-start.6
  7.4 0.9 copy-start.7
  8.3 0.8 copy-start.8
  9.0 0.8 copy-start.9
  9.8 0.7 copy-start.10
  10.5 60.8 %copy-start.1 = (bf16[1,1024,768]{2,1,0:T(8,128)(2,1)S(1)}, bf16[1,1024,768]{2,1,0:T(8,128)(2,1)}, u32[]{:S(2)}) copy-start(bf16[1,1024,768]{2,1,0:T(8,128)(2,1)} %gate_any.1) | copy-start | bytes 4718596
  10.5 60.8 %copy-start.2 = (bf16[1,1024,768]{2,1,0:T(8,128)(2,1)S(1)}, bf16[1,1024,768]{2,1,0:T(8,128)(2,1)}, u32[]{:S(2)}) copy-start(bf16[1,1024,768]{2,1,0:T(8,128)(2,1)} %up_any.1) | copy-start | bytes 4718596
  10.5 60.8 %copy-start.3 = (bf16[1,768,1024]{2,1,0:T(8,128)(2,1)S(1)}, bf16[1,768,1024]{2,1,0:T(8,128)(2,1)}, u32[]{:S(2)}) copy-start(bf16[1,768,1024]{2,1,0:T(8,128)(2,1)} %down_any.1) | copy-start | bytes 4718596

commit v2 on v0

--- a/solution.py
+++ b/solution.py
@@ -1,6 +1,10 @@
+import functools
+
 import jax
 import jax.numpy as jnp
 from jax import lax
+from jax.experimental import pallas as pl
+from jax.experimental.pallas import tpu as pltpu
 from jax.sharding import PartitionSpec as P
 
 QUERY_HEADS = 16
@@ -175,6 +179,636 @@
     return (hidden_state + mixture).astype(jnp.bfloat16)
 
 
+LANES = 128
+LOW_PART = 64
+MESH = pl.DeviceIdType.MESH
+LOG2_E = 1.4426950408889634
+
+
+def place_of(index):
+    return lax.div(index, 4), lax.rem(lax.div(index, 2), 2), lax.rem(index, 2)
+
+
+def index_of(z, x, c):
+    return (z * 2 + x) * 2 + c
+
+
+def nth_plane(k, z, planes):
+    low = jnp.minimum(z, planes - 1 - z)
+    near = k <= 2 * low
+    far = jnp.where(near, lax.div(k + 1, 2), k - low)
+    up = jnp.where(near, lax.rem(k, 2), (z < planes - 1 - z).astype(jnp.int32))
+    return z + far * (2 * up - 1)
+
+
+class Gather:
+    def __init__(self, planes, parts, send_sem, recv_sem):
+        self.planes, self.parts, self.send_sem, self.recv_sem = planes, parts, send_sem, recv_sem
+        self.me = lax.axis_index("blk")
+        self.z, self.x, self.c = place_of(self.me)
+
+    def copy(self, part, way, block):
+        z, x, c = self.z, self.x, self.c
+        target = (
+            index_of(z + 1, x, c),
+            index_of(z - 1, x, c),
+            index_of(z, 1 - x, c),
+            index_of(z, x, 1 - c),
+        )[way]
+        buf, first, rows, _ = self.parts[part]
+        piece = buf.at[block, first : first + rows]
+        return pltpu.make_async_remote_copy(
+            src_ref=piece,
+            dst_ref=piece,
+            send_sem=self.send_sem.at[part, way, block],
+            recv_sem=self.recv_sem.at[part, block],
+            device_id={"blk": target},
+            device_id_type=MESH,
+        )
+
+    def across_first(self, part):
+        return self.parts[part][3]
+
+    def arrive(self, part, block):
+        self.copy(part, 3, block).wait_recv()
+
+    def along_z(self, part, plane, block, act):
+        up = jnp.logical_and(plane <= self.z, self.z < self.planes - 1)
+        down = jnp.logical_and(plane >= self.z, self.z > 0)
+
+        @pl.when(up)
+        def _():
+            act(self.copy(part, 0, block))
+
+        @pl.when(down)
+        def _():
+            act(self.copy(part, 1, block))
+
+    def start(self):
+        for part in range(len(self.parts)):
+            for way in (2, 3):
+                self.copy(part, way, self.me).start()
+            self.along_z(part, self.z, self.me, lambda copy: copy.start())
+
+    def take_first_across(self):
+        block = index_of(self.z, 1 - self.x, self.c)
+        for part in range(len(self.parts)):
+            if self.across_first(part):
+                self.arrive(part, block)
+                self.along_z(part, self.z, block, lambda copy: copy.start())
+                self.copy(part, 3, block).start()
+
+    def take_column(self, k):
+        plane = nth_plane(k, self.z, self.planes)
+        block = index_of(plane, self.x, self.c)
+        across = index_of(plane, 1 - self.x, self.c)
+        for part in range(len(self.parts)):
+            self.arrive(part, block)
+            self.along_z(part, plane, block, lambda copy: copy.start())
+            if not self.across_first(part):
+                self.copy(part, 2, block).start()
+            self.copy(part, 3, block).start()
+        for part in range(len(self.parts)):
+            if self.across_first(part):
+                self.arrive(part, across)
+                self.along_z(part, plane, across, lambda copy: copy.start())
+                self.copy(part, 3, across).start()
+
+    def take_across(self, k):
+        plane = nth_plane(k, self.z, self.planes)
+        block = index_of(plane, 1 - self.x, self.c)
+        for part in range(len(self.parts)):
+            if not self.across_first(part):
+                self.arrive(part, block)
+                self.copy(part, 3, block).start()
+
+    def take_partner(self, k, x):
+        plane = nth_plane(k, self.z, self.planes)
+        for part in range(len(self.parts)):
+            self.arrive(part, index_of(plane, x, 1 - self.c))
+
+    def finish(self):
+        @pl.loop(0, self.planes)
+        def _(plane):
+            block = index_of(plane, self.x, self.c)
+            across = index_of(plane, 1 - self.x, self.c)
+            for part in range(len(self.parts)):
+                self.along_z(part, plane, block, lambda copy: copy.wait_send())
+                self.copy(part, 3, block).wait_send()
+                self.copy(part, 3, across).wait_send()
+                if self.across_first(part):
+                    self.along_z(part, plane, across, lambda copy: copy.wait_send())
+                else:
+                    self.copy(part, 2, block).wait_send()
+            for part in range(len(self.parts)):
+                if self.across_first(part):
+
+                    @pl.when(plane == self.z)
+                    def _():
+                        self.copy(part, 2, block).wait_send()
+
+
+def greet(planes, z, x, c):
+    barrier = pltpu.get_barrier_semaphore()
+    for target in (index_of(z, 1 - x, c), index_of(z, x, 1 - c)):
+        pl.semaphore_signal(barrier, inc=1, device_id={"blk": target}, device_id_type=MESH)
+
+    @pl.loop(0, planes)
+    def _(plane):
+        @pl.when(plane != z)
+        def _():
+            pl.semaphore_signal(
+                barrier, inc=1, device_id={"blk": index_of(plane, x, c)}, device_id_type=MESH
+            )
+
+    pl.semaphore_wait(barrier, planes + 1)
+
+
+def columns_of(rows, tokens):
+    down = lax.broadcasted_iota(jnp.int32, (tokens, tokens), 0)
+    right = lax.broadcasted_iota(jnp.int32, (tokens, tokens), 1)
+    return [
+        jnp.sum(jnp.where(down == right, rows[i : i + 1, :], 0.0), axis=1, keepdims=True)
+        for i in range(rows.shape[0])
+    ]
+
+
+def layer_kernel(
+    planes,
+    cut_keys,
+    cut_rows,
+    q_any,
+    k_any,
+    v_any,
+    new_k_any,
+    new_v_any,
+    ids_any,
+    residual_any,
+    weight_any,
+    gain_any,
+    experts_any,
+    gates_any,
+    gate_any,
+    up_any,
+    down_any,
+    out_ref,
+    kv_buf,
+    q_in,
+    new_k_ref,
+    new_v_ref,
+    ids_in,
+    residual_ref,
+    weight_buf,
+    gain_ref,
+    experts_in,
+    gates_in,
+    gate_buf,
+    up_buf,
+    down_buf,
+    ids_ref,
+    q_buf,
+    att_buf,
+    max_buf,
+    sum_buf,
+    acc_buf,
+    hidden_ref,
+    row_buf,
+    part_buf,
+    core_out,
+    core_in,
+    across_out,
+    across_in,
+    plane_out,
+    plane_in,
+    local_sem,
+    send_sem,
+    recv_sem,
+    row_send_sem,
+    row_recv_sem,
+    back_send,
+    back_recv,
+):
+    keys = k_any.shape[0]
+    low, high = keys - cut_keys, keys + cut_keys
+    gather = Gather(
+        planes,
+        (
+            (kv_buf, low, 2 * cut_keys, True),
+            (kv_buf, 0, low, False),
+            (kv_buf, high, keys - cut_keys, False),
+        ),
+        send_sem,
+        recv_sem,
+    )
+    tokens, width = residual_ref.shape
+    row_parts = ((row_buf, cut_rows, tokens - cut_rows, False),)
+    if cut_rows:
+        row_parts = ((row_buf, 0, cut_rows, True),) + row_parts
+    row_gather = Gather(planes, row_parts, row_send_sem, row_recv_sem)
+    me, z, x, c = gather.me, gather.z, gather.x, gather.c
+    moves = (
+        (k_any, kv_buf.at[me, 0:keys]),
+        (v_any, kv_buf.at[me, keys : 2 * keys]),
+        (q_any, q_in),
+        (new_k_any, new_k_ref),
+        (new_v_any, new_v_ref),
+        (ids_any, ids_in),
+        (experts_any, experts_in),
+        (gates_any, gates_in),
+        (residual_any, residual_ref),
+        (gain_any, gain_ref),
+        (weight_any, weight_buf),
+        (gate_any.at[0], gate_buf),
+        (up_any.at[0], up_buf),
+        (down_any.at[0], down_buf),
+    )
+    loads = [
+        pltpu.make_async_copy(source, target, local_sem.at[i])
+        for i, (source, target) in enumerate(moves)
+    ]
+    for load in loads[:10]:
+        load.start()
+    greet(planes, z, x, c)
+    for load in loads[:2]:
+        load.wait()
+    gather.start()
+    for load in loads[10:]:
+        load.start()
+    for load in loads[2:10]:
+        load.wait()
+
+    chunks, chunk_rows, _ = q_buf.shape
+    heads = chunk_rows // tokens
+    chunks_per_group = chunks // KEY_VALUE_HEADS
+    factor = HEAD_SIZE ** (-0.5) * LOG2_E
+
+    lane = lax.broadcasted_iota(jnp.int32, (tokens, LANES), 1)
+    ids = jnp.full((tokens, LANES), -1.0, jnp.float32)
+    for choice, column in enumerate(columns_of(ids_in[...].astype(jnp.float32), tokens)):
+        ids = jnp.where(lane == choice, column, ids)
+    ids_ref[...] = ids
+
+    for chunk in range(chunks):
+        group = chunk // chunks_per_group
+        lanes = slice(group * HEAD_SIZE, (group + 1) * HEAD_SIZE)
+        for head in range(heads):
+            at = (chunk * heads + head) * HEAD_SIZE
+            q_buf[chunk, head * tokens : (head + 1) * tokens, :] = q_in[:, at : at + HEAD_SIZE]
+        scores = lax.dot_general(
+            q_buf[chunk],
+            new_k_ref[:, lanes],
+            (((1,), (1,)), ((), ())),
+            preferred_element_type=jnp.float32,
+        )
+        row = lax.rem(lax.broadcasted_iota(jnp.int32, scores.shape, 0), tokens)
+        key = lax.broadcasted_iota(jnp.int32, scores.shape, 1)
+        scores = jnp.where(key <= row, scores, -jnp.inf)
+        top = jnp.max(scores, axis=1, keepdims=True)
+        weights = jnp.exp2((scores - top) * factor)
+        max_buf[chunk] = top
+        sum_buf[chunk] = jnp.sum(weights, axis=1, keepdims=True)
+        acc_buf[chunk] = jnp.dot(
+            weights.astype(jnp.bfloat16), new_v_ref[:, lanes], preferred_element_type=jnp.float32
+        )
+    gather.take_first_across()
+
+    @pl.loop(0, 4 * (planes + 1))
+    def _(step):
+        k, kind = lax.div(step, 4), lax.rem(step, 4)
+        late = lax.div(kind, 2)
+        valid = jnp.logical_or(
+            jnp.logical_and(late == 0, k < planes), jnp.logical_and(late == 1, k > 0)
+        )
+
+        @pl.when(valid)
+        def _():
+            place = k - late
+            plane = nth_plane(place, z, planes)
+
+            @pl.when(jnp.logical_and(kind == 0, k > 0))
+            def _():
+                gather.take_column(k)
+
+            @pl.when(kind == 1)
+            def _():
+                gather.take_partner(place, x)
+
+            @pl.when(kind == 2)
+            def _():
+                gather.take_across(place)
+
+            @pl.when(kind == 3)
+            def _():
+                gather.take_partner(place, 1 - x)
+
+            other_core = lax.rem(kind, 2)
+            block = index_of(
+                plane,
+                x + late * (1 - 2 * x),
+                c + other_core * (1 - 2 * c),
+            )
+            named = jnp.sum(
+                jnp.where(ids_ref[...] == block.astype(jnp.float32), 1.0, 0.0),
+                axis=1,
+                keepdims=True,
+            )
+            named = jnp.concatenate([named] * heads, axis=0) > 0.5
+            for chunk in range(chunks):
+                group = chunk // chunks_per_group
+                lanes = slice(group * HEAD_SIZE, (group + 1) * HEAD_SIZE)
+                scores = lax.dot_general(
+                    q_buf[chunk],
+                    kv_buf[block, 0:keys, lanes],
+                    (((1,), (1,)), ((), ())),
+                    preferred_element_type=jnp.float32,
+                )
+                before = max_buf[chunk]
+                top = jnp.maximum(before, jnp.max(scores, axis=1, keepdims=True))
+                weights = jnp.exp2((scores - top) * factor)
+                scale = jnp.where(named, jnp.exp2((before - top) * factor), 1.0)
+                total = jnp.sum(weights, axis=1, keepdims=True)
+                mixed = jnp.dot(
+                    weights.astype(jnp.bfloat16),
+                    kv_buf[block, keys : 2 * keys, lanes],
+                    preferred_element_type=jnp.float32,
+                )
+                max_buf[chunk] = jnp.where(named, top, before)
+                sum_buf[chunk] = sum_buf[chunk] * scale + jnp.where(named, total, 0.0)
+                acc_buf[chunk] = acc_buf[chunk] * scale + jnp.where(named, mixed, 0.0)
+
+            @pl.when(step == 0)
+            def _():
+                gates = gates_in[...]
+                mixing = gates / jnp.sum(gates, axis=0, keepdims=True)
+                spread = jnp.zeros((tokens, LANES), jnp.float32)
+                columns = zip(
+                    columns_of(experts_in[...].astype(jnp.float32), tokens),
+                    columns_of(mixing, tokens),
+                )
+                for expert, share in columns:
+                    expert = expert.astype(jnp.int32)
+                    hit = jnp.logical_or(lane == expert, lane == expert + LOW_PART)
+                    spread += jnp.where(hit, share, 0.0)
+                rounded = spread.astype(jnp.bfloat16).astype(jnp.float32)
+                row_buf[me, :, width:] = jnp.where(
+                    lane < LOW_PART, rounded, spread - rounded
+                ).astype(jnp.bfloat16)
+
+    for chunk in range(chunks):
+        attention = (acc_buf[chunk] / sum_buf[chunk]).astype(jnp.bfloat16)
+        for head in range(heads):
+            at = (chunk * heads + head) * HEAD_SIZE
+            att_buf[:, at : at + HEAD_SIZE] = attention[head * tokens : (head + 1) * tokens]
+    for load in loads[10:]:
+        load.wait()
+    hidden = residual_ref[...].astype(jnp.float32) + jnp.dot(
+        att_buf[...], weight_buf[...], preferred_element_type=jnp.float32
+    )
+    normed = (
+        hidden
+        * lax.rsqrt(jnp.mean(hidden * hidden, axis=-1, keepdims=True) + NORM_EPSILON)
+        * gain_ref[...]
+    )
+    row_buf[me, :, :width] = normed.astype(jnp.bfloat16)
+    row_gather.start()
+    halves = core_out.shape[1]
+    half_width = width // halves
+
+    def cols(half):
+        return slice(half * half_width, (half + 1) * half_width)
+
+    def to_core(plane, half):
+        return pltpu.make_async_remote_copy(
+            src_ref=core_out.at[plane, half],
+            dst_ref=core_in.at[plane, half],
+            send_sem=back_send.at[0, plane, half],
+            recv_sem=back_recv.at[0, plane, half],
+            device_id={"blk": index_of(z, x, 1 - c)},
+            device_id_type=MESH,
+        )
+
+    def to_across(plane, half):
+        return pltpu.make_async_remote_copy(
+            src_ref=across_out.at[plane, half],
+            dst_ref=across_in.at[plane, half],
+            send_sem=back_send.at[1, plane, half],
+            recv_sem=back_recv.at[1, plane, half],
+            device_id={"blk": index_of(z, 1 - x, c)},
+            device_id_type=MESH,
+        )
+
+    def to_plane(plane, half, sender):
+        return pltpu.make_async_remote_copy(
+            src_ref=plane_out.at[plane, half],
+            dst_ref=plane_in.at[sender, half],
+            send_sem=back_send.at[2, plane, half],
+            recv_sem=back_recv.at[2, sender, half],
+            device_id={"blk": index_of(plane, x, c)},
+            device_id_type=MESH,
+        )
+
+    hidden_ref[...] = hidden
+    row_gather.take_first_across()
+
+    @pl.loop(1, planes + 3)
+    def _(k):
+        @pl.when(k < planes)
+        def _():
+            row_gather.take_column(k)
+
+        @pl.when(k <= planes)
+        def _():
+            place = k - 1
+            plane = nth_plane(place, z, planes)
+            row_gather.take_across(place)
+            row_gather.take_partner(place, x)
+            row_gather.take_partner(place, 1 - x)
+            rows = row_buf[pl.ds(plane * 4, 4)].reshape(4 * tokens, width + LANES)
+            shares = rows[:, width:].astype(jnp.float32)
+            place_lane = lax.broadcasted_iota(jnp.int32, shares.shape, 1)
+            hit = jnp.logical_or(place_lane == me, place_lane == me + LOW_PART)
+            share = jnp.sum(jnp.where(hit, shares, 0.0), axis=1, keepdims=True)
+            rows = rows[:, :width]
+            gate_part = jnp.dot(rows, gate_buf[...], preferred_element_type=jnp.float32)
+            up_part = jnp.dot(rows, up_buf[...], preferred_element_type=jnp.float32)
+            inner = (gate_part / (1.0 + jnp.exp(-gate_part)) * up_part).astype(jnp.bfloat16)
+            for half in range(halves):
+                result = share * jnp.dot(
+                    inner, down_buf[:, cols(half)], preferred_element_type=jnp.float32
+                )
+                part_buf[pl.ds(plane * 4, 4), :, cols(half)] = result.reshape(
+                    4, tokens, half_width
+                )
+                for there in range(2):
+                    core_out[plane, half, there] = part_buf[
+                        index_of(plane, there, 1 - c), :, cols(half)
+                    ].astype(jnp.bfloat16)
+                to_core(plane, half).start()
+
+        @pl.when(jnp.logical_and(k >= 2, k <= planes + 1))
+        def _():
+            plane = nth_plane(k - 2, z, planes)
+            for half in range(halves):
+                to_core(plane, half).wait_recv()
+                across_out[plane, half] = (
+                    part_buf[index_of(plane, 1 - x, c), :, cols(half)]
+                    + core_in[plane, half, 1 - x].astype(jnp.float32)
+                ).astype(jnp.bfloat16)
+                to_across(plane, half).start()
+
+        @pl.when(k >= 3)
+        def _():
+            plane = nth_plane(k - 3, z, planes)
+            for half in range(halves):
+                to_across(plane, half).wait_recv()
+                total = (
+                    part_buf[index_of(plane, x, c), :, cols(half)]
+                    + core_in[plane, half, x].astype(jnp.float32)
+                    + across_in[plane, half].astype(jnp.float32)
+                )
+                part_buf[index_of(plane, x, c), :, cols(half)] = total
+
+                @pl.when(plane != z)
+                def _():
+                    plane_out[plane, half] = total.astype(jnp.bfloat16)
+                    to_plane(plane, half, z).start()
+
+    part_buf[me] += hidden_ref[...]
+
+    @pl.loop(0, planes)
+    def _(plane):
+        @pl.when(plane != z)
+        def _():
+            for half in range(halves):
+                to_plane(z, half, plane).wait_recv()
+                part_buf[me, :, cols(half)] += plane_in[plane, half].astype(jnp.float32)
+
+    out_ref[...] = part_buf[me].astype(jnp.bfloat16)
+
+    @pl.loop(0, planes)
+    def _(plane):
+        for half in range(halves):
+            to_core(plane, half).wait_send()
+            to_across(plane, half).wait_send()
+
+            @pl.when(plane != z)
+            def _():
+                to_plane(plane, half, z).wait_send()
+
+    gather.finish()
+    row_gather.finish()
+
+
+def gathered(*operands):
+    (
+        queries,
+        cache_keys,
+        cache_values,
+        new_keys,
+        new_values,
+        block_ids,
+        residual,
+        out_weight,
+        norm_gain,
+        expert_ids,
+        gate_scores,
+        w_gate,
+        w_up,
+        w_down,
+    ) = operands
+    parties = lax.axis_size("blk")
+    planes = parties // 4
+    tokens, width = residual.shape
+    keys, lanes = cache_keys.shape
+    bf16, f32 = jnp.bfloat16, jnp.float32
+    chunks, halves = 4, 2
+    chunk_rows = tokens * QUERY_HEADS // chunks
+    cut_keys = keys * 5 // 32 // 16 * 16
+    cut_rows = tokens // 4 // 16 * 16
+    outside = pl.BlockSpec(memory_space=pltpu.HBM)
+    inputs = (
+        queries,
+        cache_keys,
+        cache_values,
+        new_keys,
+        new_values,
+        block_ids.T,
+        residual,
+        out_weight,
+        norm_gain[None, :],
+        expert_ids.T,
+        gate_scores.T,
+        w_gate,
+        w_up,
+        w_down,
+    )
+
+    def like(array):
+        return pltpu.VMEM(array.shape, array.dtype)
+
+    back = (planes, halves, tokens, width // halves)
+    core_back = (planes, halves, 2, tokens, width // halves)
+    row_parts = 2 if cut_rows else 1
+    return pl.pallas_call(
+        functools.partial(layer_kernel, planes, cut_keys, cut_rows),
+        out_shape=jax.ShapeDtypeStruct((tokens, width), bf16),
+        in_specs=[outside] * len(inputs),
+        out_specs=pl.BlockSpec(memory_space=pltpu.VMEM),
+        scratch_shapes=[
+            pltpu.VMEM((parties, 2 * keys, lanes), bf16),
+            like(inputs[0]),
+            like(inputs[3]),
+            like(inputs[4]),
+            like(inputs[5]),
+            like(inputs[6]),
+            like(inputs[7]),
+            like(inputs[8]),
+            like(inputs[9]),
+            like(inputs[10]),
+            pltpu.VMEM(w_gate.shape[1:], bf16),
+            pltpu.VMEM(w_up.shape[1:], bf16),
+            pltpu.VMEM(w_down.shape[1:], bf16),
+            pltpu.VMEM((tokens, LANES), f32),
+            pltpu.VMEM((chunks, chunk_rows, HEAD_SIZE), bf16),
+            pltpu.VMEM((tokens, QUERY_HEADS * HEAD_SIZE), bf16),
+            pltpu.VMEM((chunks, chunk_rows, 1), f32),
+            pltpu.VMEM((chunks, chunk_rows, 1), f32),
+            pltpu.VMEM((chunks, chunk_rows, HEAD_SIZE), f32),
+            pltpu.VMEM((tokens, width), f32),
+            pltpu.VMEM((parties, tokens, width + LANES), bf16),
+            pltpu.VMEM((parties, tokens, width), f32),
+            pltpu.VMEM(core_back, bf16),
+            pltpu.VMEM(core_back, bf16),
+            pltpu.VMEM(back, bf16),
+            pltpu.VMEM(back, bf16),
+            pltpu.VMEM(back, bf16),
+            pltpu.VMEM(back, bf16),
+            pltpu.SemaphoreType.DMA((14,)),
+            pltpu.SemaphoreType.DMA((3, 4, parties)),
+            pltpu.SemaphoreType.DMA((3, parties)),
+            pltpu.SemaphoreType.DMA((row_parts, 4, parties)),
+            pltpu.SemaphoreType.DMA((row_parts, parties)),
+            pltpu.SemaphoreType.DMA((3, planes, halves)),
+            pltpu.SemaphoreType.DMA((3, planes, halves)),
+        ],
+        compiler_params=pltpu.CompilerParams(
+            collective_id=0, has_side_effects=True, vmem_limit_bytes=60 << 20
+        ),
+        name="layer",
+    )(*inputs)
+
+
+GATHER_LIMIT_BYTES = 24 << 20
+
+
+def layer(*operands):
+    parties = lax.axis_size("blk")
+    keys, values = operands[1], operands[2]
+    cache_bytes = parties * (keys.size + values.size) * keys.dtype.itemsize
+    fits = cache_bytes <= GATHER_LIMIT_BYTES and parties % 4 == 0 and parties <= LOW_PART
+    return gathered(*operands) if fits else body(*operands)
+
+
 def solution(mesh):
     placed = (
         P(("groups", "blk"), None),
@@ -193,5 +827,5 @@
         P("blk", None, None),
     )
     return jax.shard_map(
-        body, mesh=mesh, in_specs=placed, out_specs=P(("groups", "blk"), None), check_vma=False
-    )
+        layer, mesh=mesh, in_specs=placed, out_specs=P(("groups", "blk"), None), check_vma=False
+    )

time: 313 us -> 113 us (0.36); the launches traced: 308 us -> 113 us
  blocking collectives: 115 us -> 0 us
  Pallas kernels: 0 us -> 111 us
  waiting for transfers between devices: 74.1 us -> 0 us
  local copies, waits for them, and re-layouts: 47.4 us -> 1.57 us
  matrix products: 29.4 us -> 0 us
  other arithmetic: 23.5 us -> 0 us
  starting transfers between devices: 18.4 us -> 0 us
    all_to_all x2 -> x0, blocking collectives: 115 us -> none  [the longest x1 65.6 us: body(): lax.all_to_all(outgoing, 'blk', split_axis=0, concat_axis=0, tiled=True)]
    pallas_call x0 -> x1, Pallas kernels: none -> 111 us  [gathered(): pl.pallas_call(functools.partial(layer_kernel, planes, cut_keys, cut_rows...]
    all_to_all x4 -> x0, waiting for transfers between devices: 74.1 us -> none  [the longest x1 35.5 us: body(): lax.all_to_all(far_out.astype(jnp.bfloat16).reshape(senders, items, row_w...]
    dot_general x13 -> x0, matrix products: 29.4 us -> none  [the longest x4 7.43 us: partials(): lax.dot_general(group_queries, group_keys, (((1,), (1,)), ((), ())), pref...]
    gather x6 -> x0, local copies, waits for them, and re-layouts: 19 us -> none  [the longest x1 7.29 us: body(): back_out.reshape(-1, QUERY_HEADS * HEAD_SIZE)[owner_slots]]
    all_to_all x4 -> x0, starting transfers between devices: 18.4 us -> none  [the longest x1 5.22 us: body(): lax.all_to_all(far_max.reshape(senders, items, QUERY_HEADS), 'blk', split...]
    concatenate x14 -> x0, local copies, waits for them, and re-layouts: 11 us -> none  [the longest x2 4.8 us: partials(): jnp.concatenate(outputs, axis=1)]
    reduce_sum x8 -> x0, other arithmetic: 8.61 us -> none  [the longest x4 8.28 us: partials(): totals.append(jnp.sum(weights, axis=1).reshape(-1, queries_per_cluster))]
  transfers between devices with their start and end apart: 4 -> 0, of which waited for: 4 -> 0; matrix products, arithmetic and copies ran while one was open for 7% -> 0% of each run, Pallas kernels for 0% -> 0%
where the time goes in v2:
time: 113 us
  Pallas kernels  111 us (98%)
  local copies, waits for them, and re-layouts  1.57 us (1%)
    pallas_call x1, Pallas kernels, gathered(): pl.pallas_call(functools.partial(layer_kernel, planes, cut_keys, cut_rows...  111 us

profile of v2, /device:TPU:0, one launch (start us, length us, event | category | flops | bytes accessed | tf_op | source)
XLA Modules:
  0.0 112.8 jit_solution(6421197857986139935)
XLA Ops:
  0.0 111.3 %layer.1 = bf16[64,1024]{1,0:T(8,128)(2,1)} custom-call(bf16[64,2048]{1,0:T(8,128)(2,1)} %q_any.1, bf16[512,256]{1,0:T(8,128)(2,1)} %k_any.1, bf16[512,256]{1,0:T(8,128)(2,1)} %v_any.1, bf16[64,256]{1,0:T(8,128)(2,1)} %new_k_any.1, bf16[64,256]{1,0:T(8,128)(2,1)} %new_v_any.1, s32[8,64]{1,0:T(8,128)} %bitcast.4, bf16[64,1024]{1,0:T(8,128)(2,1)} %residual_any.1, ...), custom_call_target="tpu_custom_call" | custom-call | tf_op jit(solution)/shard_map/layer/pallas_call | solution.py:752
  111.3 1.6 %copy.16 = bf16[64,1024]{1,0:T(8,128)(2,1)} copy(bf16[64,1024]{1,0:T(8,128)(2,1)} %layer.1) | data formatting | bytes 262144

commit v3 on v2

--- a/solution.py
+++ b/solution.py
@@ -182,6 +182,7 @@
 LANES = 128
 LOW_PART = 64
 MESH = pl.DeviceIdType.MESH
+LOWEST = -1e30
 LOG2_E = 1.4426950408889634
 
 
@@ -335,7 +336,6 @@
 
 def layer_kernel(
     planes,
-    cut_keys,
     cut_rows,
     q_any,
     k_any,
@@ -353,7 +353,7 @@
     down_any,
     out_ref,
     kv_buf,
-    q_in,
+    q_rows,
     new_k_ref,
     new_v_ref,
     ids_in,
@@ -365,7 +365,6 @@
     gate_buf,
     up_buf,
     down_buf,
-    ids_ref,
     q_buf,
     att_buf,
     max_buf,
@@ -380,7 +379,15 @@
     across_in,
     plane_out,
     plane_in,
+    o_out,
+    o_in,
+    stat_out,
+    stat_in,
     local_sem,
+    kv_send,
+    kv_recv,
+    give_send,
+    give_recv,
     send_sem,
     recv_sem,
     row_send_sem,
@@ -389,17 +396,8 @@
     back_recv,
 ):
     keys = k_any.shape[0]
-    low, high = keys - cut_keys, keys + cut_keys
-    gather = Gather(
-        planes,
-        (
-            (kv_buf, low, 2 * cut_keys, True),
-            (kv_buf, 0, low, False),
-            (kv_buf, high, keys - cut_keys, False),
-        ),
-        send_sem,
-        recv_sem,
-    )
+    tokens = residual_ref.shape[0]
+    gather = Gather(planes, ((q_rows, 0, tokens, False),), send_sem, recv_sem)
     tokens, width = residual_ref.shape
     row_parts = ((row_buf, cut_rows, tokens - cut_rows, False),)
     if cut_rows:
@@ -407,12 +405,12 @@
     row_gather = Gather(planes, row_parts, row_send_sem, row_recv_sem)
     me, z, x, c = gather.me, gather.z, gather.x, gather.c
     moves = (
-        (k_any, kv_buf.at[me, 0:keys]),
-        (v_any, kv_buf.at[me, keys : 2 * keys]),
-        (q_any, q_in),
+        (k_any, kv_buf.at[0, 0:keys]),
+        (v_any, kv_buf.at[0, keys : 2 * keys]),
+        (q_any, q_rows.at[me, :, 0 : q_any.shape[1]]),
+        (ids_any, ids_in),
         (new_k_any, new_k_ref),
         (new_v_any, new_v_ref),
-        (ids_any, ids_in),
         (experts_any, experts_in),
         (gates_any, gates_in),
         (residual_any, residual_ref),
@@ -429,12 +427,33 @@
     for load in loads[:10]:
         load.start()
     greet(planes, z, x, c)
-    for load in loads[:2]:
+    def send_cache(to, source, target):
+        return pltpu.make_async_remote_copy(
+            src_ref=kv_buf.at[source],
+            dst_ref=kv_buf.at[target],
+            send_sem=kv_send.at[target],
+            recv_sem=kv_recv.at[target],
+            device_id={"blk": to},
+            device_id_type=MESH,
+        )
+
+    to_core_own = send_cache(index_of(z, x, 1 - c), 0, 1)
+    to_across_own = send_cache(index_of(z, 1 - x, c), 0, 2)
+    to_core_across = send_cache(index_of(z, x, 1 - c), 2, 3)
+    for load in loads[:4]:
         load.wait()
-    gather.start()
+    to_across_own.start()
+    to_core_own.start()
+    lane = lax.broadcasted_iota(jnp.int32, (tokens, LANES), 1)
+    ids = jnp.full((tokens, LANES), -1.0, jnp.float32)
+    for choice, column in enumerate(columns_of(ids_in[...].astype(jnp.float32), tokens)):
+        ids = jnp.where(lane == choice, column, ids)
+    features = q_any.shape[1]
+    q_rows[me, :, features:] = ids.astype(jnp.bfloat16)
+    gather.along_z(0, z, me, lambda copy: copy.start())
     for load in loads[10:]:
         load.start()
-    for load in loads[2:10]:
+    for load in loads[4:10]:
         load.wait()
 
     chunks, chunk_rows, _ = q_buf.shape
@@ -442,18 +461,22 @@
     chunks_per_group = chunks // KEY_VALUE_HEADS
     factor = HEAD_SIZE ** (-0.5) * LOG2_E
 
-    lane = lax.broadcasted_iota(jnp.int32, (tokens, LANES), 1)
-    ids = jnp.full((tokens, LANES), -1.0, jnp.float32)
-    for choice, column in enumerate(columns_of(ids_in[...].astype(jnp.float32), tokens)):
-        ids = jnp.where(lane == choice, column, ids)
-    ids_ref[...] = ids
-
+    max_buf[...] = jnp.full(max_buf.shape, LOWEST, jnp.float32)
+    sum_buf[...] = jnp.zeros(sum_buf.shape, jnp.float32)
+    acc_buf[...] = jnp.zeros(acc_buf.shape, jnp.float32)
+
+    def stack_heads(source):
+        for chunk in range(chunks):
+            for head in range(heads):
+                at = (chunk * heads + head) * HEAD_SIZE
+                q_buf[chunk, head * tokens : (head + 1) * tokens, :] = q_rows[
+                    source, :, at : at + HEAD_SIZE
+                ]
+
+    stack_heads(me)
     for chunk in range(chunks):
         group = chunk // chunks_per_group
         lanes = slice(group * HEAD_SIZE, (group + 1) * HEAD_SIZE)
-        for head in range(heads):
-            at = (chunk * heads + head) * HEAD_SIZE
-            q_buf[chunk, head * tokens : (head + 1) * tokens, :] = q_in[:, at : at + HEAD_SIZE]
         scores = lax.dot_general(
             q_buf[chunk],
             new_k_ref[:, lanes],
@@ -465,50 +488,79 @@
         scores = jnp.where(key <= row, scores, -jnp.inf)
         top = jnp.max(scores, axis=1, keepdims=True)
         weights = jnp.exp2((scores - top) * factor)
-        max_buf[chunk] = top
-        sum_buf[chunk] = jnp.sum(weights, axis=1, keepdims=True)
-        acc_buf[chunk] = jnp.dot(
+        max_buf[z, chunk] = top
+        sum_buf[z, chunk] = jnp.sum(weights, axis=1, keepdims=True)
+        acc_buf[z, chunk] = jnp.dot(
             weights.astype(jnp.bfloat16), new_v_ref[:, lanes], preferred_element_type=jnp.float32
         )
-    gather.take_first_across()
-
-    @pl.loop(0, 4 * (planes + 1))
+    def give_back(plane, what):
+        source, target = ((o_out, o_in), (stat_out, stat_in))[what]
+        return lambda sender: pltpu.make_async_remote_copy(
+            src_ref=source.at[plane],
+            dst_ref=target.at[sender],
+            send_sem=give_send.at[what, plane],
+            recv_sem=give_recv.at[what, sender],
+            device_id={"blk": index_of(plane, x, c)},
+            device_id_type=MESH,
+        )
+
+    def take_queries(k):
+        plane = nth_plane(k, z, planes)
+        block = index_of(plane, x, c)
+        gather.arrive(0, block)
+        gather.along_z(0, plane, block, lambda copy: copy.start())
+
+    last = planes - 1
+
+    @pl.loop(0, 4 * planes)
     def _(step):
-        k, kind = lax.div(step, 4), lax.rem(step, 4)
-        late = lax.div(kind, 2)
-        valid = jnp.logical_or(
-            jnp.logical_and(late == 0, k < planes), jnp.logical_and(late == 1, k > 0)
-        )
-
-        @pl.when(valid)
-        def _():
-            place = k - late
-            plane = nth_plane(place, z, planes)
-
-            @pl.when(jnp.logical_and(kind == 0, k > 0))
+        pair, other_core = lax.div(step, 2), lax.rem(step, 2)
+        middle = pair < 2 * planes - 3
+        first_half = jnp.logical_or(pair < last, pair == 2 * planes - 3)
+        k = jnp.where(
+            pair < last,
+            pair,
+            jnp.where(middle, pair - (planes - 2), jnp.where(pair < 2 * planes - 1, last, 0)),
+        )
+        far = jnp.where(first_half, 0, 1)
+        if True:
+            plane = nth_plane(k, z, planes)
+            owner = index_of(plane, x, c)
+
+            @pl.when(other_core == 0)
             def _():
-                gather.take_column(k)
-
-            @pl.when(kind == 1)
+                @pl.when(jnp.logical_and(pair > 0, pair < last))
+                def _():
+                    take_queries(pair)
+
+                @pl.when(pair == last)
+                def _():
+                    to_across_own.wait_recv()
+                    to_core_across.start()
+
+                @pl.when(pair == 2 * planes - 4)
+                def _():
+                    take_queries(last)
+
+                stack_heads(owner)
+
+            @pl.when(step == 1)
             def _():
-                gather.take_partner(place, x)
-
-            @pl.when(kind == 2)
+                to_core_own.wait_recv()
+
+            @pl.when(step == 2 * last + 1)
             def _():
-                gather.take_across(place)
-
-            @pl.when(kind == 3)
-            def _():
-                gather.take_partner(place, 1 - x)
-
-            other_core = lax.rem(kind, 2)
+                to_core_across.wait_recv()
+
+            slot = 2 * far + other_core
             block = index_of(
-                plane,
-                x + late * (1 - 2 * x),
+                z,
+                x + far * (1 - 2 * x),
                 c + other_core * (1 - 2 * c),
             )
+            chosen = q_rows[owner, :, features:].astype(jnp.float32)
             named = jnp.sum(
-                jnp.where(ids_ref[...] == block.astype(jnp.float32), 1.0, 0.0),
+                jnp.where(chosen == block.astype(jnp.float32), 1.0, 0.0),
                 axis=1,
                 keepdims=True,
             )
@@ -518,23 +570,41 @@
                 lanes = slice(group * HEAD_SIZE, (group + 1) * HEAD_SIZE)
                 scores = lax.dot_general(
                     q_buf[chunk],
-                    kv_buf[block, 0:keys, lanes],
+                    kv_buf[slot, 0:keys, lanes],
                     (((1,), (1,)), ((), ())),
                     preferred_element_type=jnp.float32,
                 )
-                before = max_buf[chunk]
+                before = max_buf[plane, chunk]
                 top = jnp.maximum(before, jnp.max(scores, axis=1, keepdims=True))
                 weights = jnp.exp2((scores - top) * factor)
                 scale = jnp.where(named, jnp.exp2((before - top) * factor), 1.0)
                 total = jnp.sum(weights, axis=1, keepdims=True)
                 mixed = jnp.dot(
                     weights.astype(jnp.bfloat16),
-                    kv_buf[block, keys : 2 * keys, lanes],
+                    kv_buf[slot, keys : 2 * keys, lanes],
                     preferred_element_type=jnp.float32,
                 )
-                max_buf[chunk] = jnp.where(named, top, before)
-                sum_buf[chunk] = sum_buf[chunk] * scale + jnp.where(named, total, 0.0)
-                acc_buf[chunk] = acc_buf[chunk] * scale + jnp.where(named, mixed, 0.0)
+                max_buf[plane, chunk] = jnp.where(named, top, before)
+                sum_buf[plane, chunk] = sum_buf[plane, chunk] * scale + jnp.where(named, total, 0.0)
+                acc_buf[plane, chunk] = acc_buf[plane, chunk] * scale + jnp.where(named, mixed, 0.0)
+
+            @pl.when(jnp.logical_and(slot == 3, k > 0))
+            def _():
+                stat = jnp.zeros((tokens, LANES), jnp.float32)
+                for chunk in range(chunks):
+                    for head in range(heads):
+                        number = chunk * heads + head
+                        part = slice(head * tokens, (head + 1) * tokens)
+                        stat = jnp.where(lane == number, max_buf[plane, chunk, part], stat)
+                        stat = jnp.where(
+                            lane == LOW_PART + number, sum_buf[plane, chunk, part], stat
+                        )
+                        o_out[plane, :, number * HEAD_SIZE : (number + 1) * HEAD_SIZE] = acc_buf[
+                            plane, chunk, part
+                        ].astype(jnp.bfloat16)
+                stat_out[plane] = stat
+                give_back(plane, 0)(z).start()
+                give_back(plane, 1)(z).start()
 
             @pl.when(step == 0)
             def _():
@@ -554,11 +624,33 @@
                     lane < LOW_PART, rounded, spread - rounded
                 ).astype(jnp.bfloat16)
 
-    for chunk in range(chunks):
-        attention = (acc_buf[chunk] / sum_buf[chunk]).astype(jnp.bfloat16)
-        for head in range(heads):
-            at = (chunk * heads + head) * HEAD_SIZE
-            att_buf[:, at : at + HEAD_SIZE] = attention[head * tokens : (head + 1) * tokens]
+    stat = jnp.zeros((tokens, LANES), jnp.float32)
+    for number in range(chunks * heads):
+        chunk, head = number // heads, number % heads
+        part = slice(head * tokens, (head + 1) * tokens)
+        stat = jnp.where(lane == number, max_buf[z, chunk, part], stat)
+    stat_out[z] = stat
+    for k in range(1, planes):
+        plane = nth_plane(jnp.int32(k), z, planes)
+        give_back(z, 0)(plane).wait_recv()
+        give_back(z, 1)(plane).wait_recv()
+        stat_out[z] = jnp.maximum(stat_out[z], stat_in[plane])
+    tops = stat_out[z]
+    for number in range(chunks * heads):
+        chunk, head = number // heads, number % heads
+        part = slice(head * tokens, (head + 1) * tokens)
+        at = slice(number * HEAD_SIZE, (number + 1) * HEAD_SIZE)
+        top = tops[:, number : number + 1]
+        scale = jnp.exp2((max_buf[z, chunk, part] - top) * factor)
+        total = sum_buf[z, chunk, part] * scale
+        mixed = acc_buf[z, chunk, part] * scale
+        for k in range(1, planes):
+            plane = nth_plane(jnp.int32(k), z, planes)
+            theirs = stat_in[plane]
+            scale = jnp.exp2((theirs[:, number : number + 1] - top) * factor)
+            total += theirs[:, LOW_PART + number : LOW_PART + number + 1] * scale
+            mixed += o_in[plane, :, at].astype(jnp.float32) * scale
+        att_buf[:, at] = (mixed / total).astype(jnp.bfloat16)
     for load in loads[10:]:
         load.wait()
     hidden = residual_ref[...].astype(jnp.float32) + jnp.dot(
@@ -695,7 +787,17 @@
             def _():
                 to_plane(plane, half, z).wait_send()
 
-    gather.finish()
+    @pl.loop(0, planes)
+    def _(plane):
+        gather.along_z(0, plane, index_of(plane, x, c), lambda copy: copy.wait_send())
+
+        @pl.when(plane != z)
+        def _():
+            give_back(plane, 0)(z).wait_send()
+            give_back(plane, 1)(z).wait_send()
+
+    for copy in (to_core_own, to_across_own, to_core_across):
+        copy.wait_send()
     row_gather.finish()
 
 
@@ -723,7 +825,6 @@
     bf16, f32 = jnp.bfloat16, jnp.float32
     chunks, halves = 4, 2
     chunk_rows = tokens * QUERY_HEADS // chunks
-    cut_keys = keys * 5 // 32 // 16 * 16
     cut_rows = tokens // 4 // 16 * 16
     outside = pl.BlockSpec(memory_space=pltpu.HBM)
     inputs = (
@@ -750,13 +851,13 @@
     core_back = (planes, halves, 2, tokens, width // halves)
     row_parts = 2 if cut_rows else 1
     return pl.pallas_call(
-        functools.partial(layer_kernel, planes, cut_keys, cut_rows),
+        functools.partial(layer_kernel, planes, cut_rows),
         out_shape=jax.ShapeDtypeStruct((tokens, width), bf16),
         in_specs=[outside] * len(inputs),
         out_specs=pl.BlockSpec(memory_space=pltpu.VMEM),
         scratch_shapes=[
-            pltpu.VMEM((parties, 2 * keys, lanes), bf16),
-            like(inputs[0]),
+            pltpu.VMEM((4, 2 * keys, lanes), bf16),
+            pltpu.VMEM((parties, tokens, queries.shape[1] + LANES), bf16),
             like(inputs[3]),
             like(inputs[4]),
             like(inputs[5]),
@@ -768,12 +869,11 @@
             pltpu.VMEM(w_gate.shape[1:], bf16),
             pltpu.VMEM(w_up.shape[1:], bf16),
             pltpu.VMEM(w_down.shape[1:], bf16),
-            pltpu.VMEM((tokens, LANES), f32),
             pltpu.VMEM((chunks, chunk_rows, HEAD_SIZE), bf16),
             pltpu.VMEM((tokens, QUERY_HEADS * HEAD_SIZE), bf16),
-            pltpu.VMEM((chunks, chunk_rows, 1), f32),
-            pltpu.VMEM((chunks, chunk_rows, 1), f32),
-            pltpu.VMEM((chunks, chunk_rows, HEAD_SIZE), f32),
+            pltpu.VMEM((planes, chunks, chunk_rows, 1), f32),
+            pltpu.VMEM((planes, chunks, chunk_rows, 1), f32),
+            pltpu.VMEM((planes, chunks, chunk_rows, HEAD_SIZE), f32),
             pltpu.VMEM((tokens, width), f32),
             pltpu.VMEM((parties, tokens, width + LANES), bf16),
             pltpu.VMEM((parties, tokens, width), f32),
@@ -783,9 +883,17 @@
             pltpu.VMEM(back, bf16),
             pltpu.VMEM(back, bf16),
             pltpu.VMEM(back, bf16),
+            pltpu.VMEM((planes,) + queries.shape, bf16),
+            pltpu.VMEM((planes,) + queries.shape, bf16),
+            pltpu.VMEM((planes, tokens, LANES), f32),
+            pltpu.VMEM((planes, tokens, LANES), f32),
             pltpu.SemaphoreType.DMA((14,)),
-            pltpu.SemaphoreType.DMA((3, 4, parties)),
-            pltpu.SemaphoreType.DMA((3, parties)),
+            pltpu.SemaphoreType.DMA((4,)),
+            pltpu.SemaphoreType.DMA((4,)),
+            pltpu.SemaphoreType.DMA((2, planes)),
+            pltpu.SemaphoreType.DMA((2, planes)),
+            pltpu.SemaphoreType.DMA((1, 4, parties)),
+            pltpu.SemaphoreType.DMA((1, parties)),
             pltpu.SemaphoreType.DMA((row_parts, 4, parties)),
             pltpu.SemaphoreType.DMA((row_parts, parties)),
             pltpu.SemaphoreType.DMA((3, planes, halves)),
@@ -805,7 +913,7 @@
     parties = lax.axis_size("blk")
     keys, values = operands[1], operands[2]
     cache_bytes = parties * (keys.size + values.size) * keys.dtype.itemsize
-    fits = cache_bytes <= GATHER_LIMIT_BYTES and parties % 4 == 0 and parties <= LOW_PART
+    fits = cache_bytes <= GATHER_LIMIT_BYTES and parties % 4 == 0 and parties >= 12 and parties <= LOW_PART
     return gathered(*operands) if fits else body(*operands)
 
 

time: 113 us -> 109 us (0.965)
  Pallas kernels: 111 us -> 107 us
    pallas_call x1, Pallas kernels: 111 us -> 107 us  [gathered(): pl.pallas_call(functools.partial(layer_kernel, planes, cut_rows), out_sha...]
where the time goes in v3:
time: 109 us
  Pallas kernels  107 us (98%)
  local copies, waits for them, and re-layouts  1.57 us (1%)
    pallas_call x1, Pallas kernels, gathered(): pl.pallas_call(functools.partial(layer_kernel, planes, cut_rows), out_sha...  107 us

profile of v3, /device:TPU:0, one launch (start us, length us, event | category | flops | bytes accessed | tf_op | source)
XLA Modules:
  0.0 108.8 jit_solution(7260200762369780074)
XLA Ops:
  0.0 107.2 %layer.1 = bf16[64,1024]{1,0:T(8,128)(2,1)} custom-call(bf16[64,2048]{1,0:T(8,128)(2,1)} %q_any.1, bf16[512,256]{1,0:T(8,128)(2,1)} %k_any.1, bf16[512,256]{1,0:T(8,128)(2,1)} %v_any.1, bf16[64,256]{1,0:T(8,128)(2,1)} %new_k_any.1, bf16[64,256]{1,0:T(8,128)(2,1)} %new_v_any.1, s32[8,64]{1,0:T(8,128)} %bitcast.4, bf16[64,1024]{1,0:T(8,128)(2,1)} %residual_any.1, ...), custom_call_target="tpu_custom_call" | custom-call | tf_op jit(solution)/shard_map/layer/pallas_call | solution.py:853
  107.2 1.6 %copy.16 = bf16[64,1024]{1,0:T(8,128)(2,1)} copy(bf16[64,1024]{1,0:T(8,128)(2,1)} %layer.1) | data formatting | bytes 262144
